TPU v7x, 32 devices: a whole 2x2x4 slice. The times are simulated.
32 devices in a mesh: row: 8 (over z, y), col: 2 (over x), fiber: 2 (over core).
Axes of the slice: x: 2, y: 2, z: 4, core: 2. Of those that a mesh axis runs over, the one named last changes fastest.
Arguments:
- a_panels: float32 [3072, 2, 2, 768], P(('row', 'col'), 'fiber'), may hold values from -12 to 12
- b_panels: float32 [2, 2, 768, 2048], P('fiber', None, 'row', 'col'), may hold values from -0.15625 to 0.15625
- a_pattern: int32 [24, 2, 2, 6], P('row', 'fiber'), may hold values 0 or 1
- c_pattern: int32 [24, 16], P('row', 'col'), may hold values 0 or 1
Outputs:
- scaled: float32 [3072, 2048], P(('row', 'fiber'), 'col')
All inputs are finite; a program needn't handle non-finite values. No bound on the sum of `a_pattern` or of `c_pattern` on one device may be relied on, other than what follows from the above.
Results may differ from a plain program's by a relative error of at most 0.00013.
Values sent between devices are 32-bit elements; how exact they have to be, the bound alone decides.
No kernel may reach another device: no remote copies, remote signals or barrier semaphores. Data moves between devices by JAX's collectives and lax.ppermute only.
A program may use at most 64 MiB of HBM per device.

v0:
```python
import functools

import jax
import jax.numpy as jnp
from jax import lax
from jax.experimental import pallas as pl
from jax.experimental.pallas import tpu as pltpu
from jax.sharding import PartitionSpec as P


BLK = 128


EPS = 1e-06
TILE = 256
CHUNK = 256


LINE = (0, 1, 3, 2)


def line_pairs(shift):
    size = len(LINE)
    return [
        (LINE[i] * 2 + y, LINE[(i + shift) % size] * 2 + y) for i in range(size) for y in range(2)
    ]


def line_at(z, step):
    place = jnp.where(z < 2, z, 5 - z)
    place = (place + step + len(LINE)) % len(LINE)
    return jnp.where(place < 2, place, 5 - place)


def all_sum(value, axis_name):
    size = lax.axis_size(axis_name)
    stride = 1
    while stride < size:
        rest = size // stride
        radix = next(p for p in range(2, rest + 1) if rest % p == 0)
        total = value
        for turn in range(1, radix):
            pairs = []
            for i in range(size):
                digit = i // stride % radix
                pairs.append((i, i + ((digit + turn) % radix - digit) * stride))
            total = total + lax.ppermute(value, axis_name, pairs)
        value = total
        stride *= radix
    return value


def gathered(a_panels, b_panels, a_pattern, c_pattern):
    _, _, sections, width = a_panels.shape
    block_rows, width_blocks = a_pattern.shape[0], a_pattern.shape[3]
    columns = b_panels.shape[3]
    local_rows = block_rows * BLK
    n_row, fibers = lax.axis_size("row"), lax.axis_size("fiber")
    share = local_rows // fibers
    total = jnp.zeros((local_rows, columns), jnp.float32)
    for section in range(sections):
        block = lax.all_gather(a_panels[:, 0, section, :], "col", axis=0, tiled=True)
        keep = a_pattern[:, 0, section, :].astype(jnp.float32)
        left = block.reshape(block_rows, BLK, width_blocks, BLK) * keep[:, None, :, None]
        right = lax.all_gather(b_panels[0, section], "row", axis=0, tiled=True)
        total = total + jnp.dot(
            left.reshape(local_rows, width),
            right,
            precision=lax.Precision.HIGH,
            preferred_element_type=jnp.float32,
        )
    keep = jnp.broadcast_to(
        c_pattern.astype(jnp.float32)[:, None, :, None],
        (block_rows, BLK, columns // BLK, BLK),
    ).reshape(local_rows, columns)
    merged = lax.psum_scatter(total, "fiber", scatter_dimension=0, tiled=True)
    product = merged * lax.dynamic_slice_in_dim(keep, lax.axis_index("fiber") * share, share, 0)
    inflated = product * product
    sums = all_sum(all_sum(jnp.sum(inflated, axis=0, keepdims=True), "fiber"), "row")
    return inflated / (sums / (share * fibers * n_row) + EPS)


def split(value):
    high = value.astype(jnp.bfloat16)
    low = (value - high.astype(jnp.float32)).astype(jnp.bfloat16)
    return high, low


def product3(a_high, a_low, b_high, b_low):
    def dot(x, y):
        return jnp.dot(x, y, preferred_element_type=jnp.float32)

    return dot(a_high, b_high) + (dot(a_high, b_low) + dot(a_low, b_high))


def left_kernel(steps, pattern, source, mine, other, turned):
    rows, _, sections, width = source.shape
    n_row, row = lax.axis_size("row"), lax.axis_index("row")
    depth = width // n_row
    group = 64
    for g in range(rows // group):
        part = pl.ds(g * group, group)
        block_row = (lax.axis_index("col") * rows + g * group) // BLK
        for s in range(sections):
            kept = []
            for w in range(width // BLK):
                keep = pattern[block_row, 0, s, w]
                piece = source[part, 0, s, pl.ds(w * BLK, BLK)]
                kept.append(jnp.where(keep != 0, piece, 0.0))
            value = jnp.concatenate(kept, axis=1)
            for r in range(n_row):
                turned[r, s, part, :] = value[:, r * depth : (r + 1) * depth]
        for out, parity in ((mine, row % 2), (other, 1 - row % 2)):
            owners = [line_at(row // 2, step) * 2 + parity for step in steps]
            pieces = [turned[r, s, part, :] for r in owners for s in range(sections)]
            out[part, :] = jnp.concatenate(pieces, axis=1)


def order_kernel(cuts, *refs):
    pieces, outs = refs[:4], refs[4:]
    rows = pieces[0].shape[0]
    flip = lax.axis_index("col") ^ lax.axis_index("fiber")
    for p, piece in enumerate(pieces):
        y, x = divmod(p, 2)
        start = pl.multiple_of((y + 2 * (x ^ flip)) * rows, rows)
        for i, (low_end, high_end) in enumerate(cuts):
            high, low = split(piece[:, low_end:high_end])
            outs[2 * i][pl.ds(start, rows), :] = high
            outs[2 * i + 1][pl.ds(start, rows), :] = low


def group_kernel(count, *refs):
    high, low, *rest = refs
    shards, (*near, out, b_high, b_low) = rest[:count], rest[count:]
    _, sections, depth, columns = shards[0].shape
    for i in range(count * sections):
        part = pl.ds(i * depth, depth)
        b_high[part, :], b_low[part, :] = split(shards[i // sections][0, i % sections])
    for t in range(columns // TILE):
        tile = pl.ds(t * TILE, TILE)
        total = product3(high[...], low[...], b_high[:, tile], b_low[:, tile])
        out[:, tile] = near[0][:, tile] + total if near else total


def far_kernel(first, high, low, near, shard, kept, sent, b_high, b_low):
    _, sections, depth, columns = shard.shape
    rows = kept.shape[1]
    for s in range(sections):
        part = pl.ds(s * depth, depth)
        b_high[part, :], b_low[part, :] = split(shard[0, s])
    value = product3(high[...], low[...], b_high[...], b_low[...])
    for q in range(4):
        out = sent if q >= 2 else kept
        block = pl.ds(q * rows, rows)
        out[q % 2] = near[block, first : first + columns] + value[q * rows : (q + 1) * rows]


def fold_kernel(kept, received, mine, other):
    mine[...] = kept[0] + received[0]
    other[...] = kept[1] + received[1]


def square_kernel(first, pattern, mine, received, *refs):
    *before, squares, sums = refs
    share, columns = mine.shape
    fiber = lax.axis_index("fiber")
    group = 64
    for w in range(columns // BLK):
        tile = pl.ds(w * BLK, BLK)
        total = jnp.zeros((8, BLK), jnp.float32)
        for g in range(share // group):
            keep = pattern[(fiber * share + g * group) // BLK, first // BLK + w]
            part = pl.ds(g * group, group)
            value = mine[part, tile] + received[part, tile]
            value = jnp.where(keep != 0, value, 0.0)
            value = value * value
            squares[part, tile] = value
            total += jnp.sum(value.reshape(group // 8, 8, BLK), axis=0)
        sums[:, pl.ds(first + w * BLK, BLK)] = jnp.sum(total, axis=0, keepdims=True)
    for old in before:
        sums[:, pl.ds(0, first)] = old[...]


def scale_kernel(row_total, sums, *refs):
    *chunks, out = refs
    first = 0
    for chunk in chunks:
        tile = pl.ds(first, chunk.shape[1])
        out[:, tile] = chunk[...] / (sums[:, tile] / row_total + EPS)
        first += chunk.shape[1]


def together(*values):
    return lax.optimization_barrier(values)


VMEM = pl.BlockSpec(memory_space=pltpu.VMEM)
SMEM = pl.BlockSpec(memory_space=pltpu.SMEM)


def call(kernel, out_shapes, specs, scratch=(), flops=0):
    def run(*args):
        moved = sum(a.size * a.dtype.itemsize for a in (*args, *out_shapes))
        return pl.pallas_call(
            kernel,
            out_shape=out_shapes,
            in_specs=specs,
            out_specs=[VMEM] * len(out_shapes),
            scratch_shapes=scratch,
            cost_estimate=pl.CostEstimate(flops=flops, bytes_accessed=moved, transcendentals=0),
            compiler_params=pltpu.CompilerParams(vmem_limit_bytes=16 * 2**20),
        )(*args)

    return run


def local(a_panels, b_panels, a_pattern, c_pattern):
    rows, _, sections, width = a_panels.shape
    depth, columns = b_panels.shape[2:]
    n_row, n_col, fibers = (lax.axis_size(name) for name in ("row", "col", "fiber"))
    local_rows = rows * n_col
    share = local_rows // fibers
    if (n_row, n_col, fibers, sections) != (8, 2, 2, 2):
        return gathered(a_panels, b_panels, a_pattern, c_pattern)

    f32, bf16 = jnp.float32, jnp.bfloat16
    shape = jax.ShapeDtypeStruct
    shard_depth = sections * depth
    half = width * sections // 2
    plane_rows = 4 * rows

    down = lax.ppermute(b_panels, "row", line_pairs(1))
    up = lax.ppermute(b_panels, "row", line_pairs(-1))

    steps = (-1, 1, 0, 2)
    mine, other = call(
        functools.partial(left_kernel, steps),
        [shape((rows, half), f32)] * 2,
        [SMEM, VMEM],
        [pltpu.VMEM((n_row, sections, rows, depth), f32)],
    )(a_pattern, a_panels)
    swap = [(0, 1), (1, 0)]
    swap_y = [(r, r ^ 1) for r in range(n_row)]
    swap_both = [(r * 2 + c, (r ^ 1) * 2 + 1 - c) for r in range(n_row) for c in range(2)]
    from_x = lax.ppermute(mine, "col", swap)
    from_y = lax.ppermute(other, "row", swap_y)
    from_both = lax.ppermute(other, ("row", "col"), swap_both)
    cuts = ((0, 2 * shard_depth), (2 * shard_depth, 3 * shard_depth), (3 * shard_depth, half))
    near_high, near_low, own_high, own_low, far_high, far_low = call(
        functools.partial(order_kernel, cuts),
        [shape((plane_rows, b - a), bf16) for a, b in cuts for _ in range(2)],
        [VMEM] * 4,
    )(mine, from_x, from_y, from_both)

    def product(high, low, *shards_and_near):
        depth_here = high.shape[1]
        factor = pltpu.VMEM((depth_here, columns), bf16)
        (total,) = call(
            functools.partial(group_kernel, depth_here // shard_depth),
            [shape((plane_rows, columns), f32)],
            [VMEM] * (2 + len(shards_and_near)),
            [factor, factor],
            6 * plane_rows * columns * depth_here,
        )(high, low, *shards_and_near)
        return total

    far = [
        lax.ppermute(down[..., j * CHUNK : (j + 1) * CHUNK], "row", line_pairs(1))
        for j in range(columns // CHUNK)
    ]
    near = product(own_high, own_low, b_panels)
    near = product(near_high, near_low, down, up, near)

    ends = []
    for j, shard in enumerate(far):
        if ends:
            shard, _ = together(shard, ends[-1])
        factor = pltpu.VMEM((shard_depth, CHUNK), bf16)
        kept, sent = call(
            functools.partial(far_kernel, j * CHUNK),
            [shape((2, rows, CHUNK), f32)] * 2,
            [VMEM] * 4,
            [factor, factor],
            6 * plane_rows * CHUNK * shard_depth,
        )(far_high, far_low, near, shard)
        received = lax.ppermute(sent, "fiber", swap)
        stays, goes = call(fold_kernel, [shape((rows, CHUNK), f32)] * 2, [VMEM] * 2)(kept, received)
        ends.append(goes)
        far[j] = stays, lax.ppermute(goes, "row", swap_y)
    squares, sums = [], []
    for j, (stays, received) in enumerate(far):
        received, _ = together(received, ends[-1])
        square, total = call(
            functools.partial(square_kernel, j * CHUNK),
            [shape((rows, CHUNK), f32), shape((1, (j + 1) * CHUNK), f32)],
            [SMEM] + [VMEM] * (2 + len(sums)),
        )(c_pattern, stays, received, *sums)
        squares.append(square)
        sums = [total]
    total = all_sum(all_sum(sums[0], "fiber"), "row")
    (out,) = call(
        functools.partial(scale_kernel, share * fibers * n_row),
        [shape((share, columns), f32)],
        [VMEM] * (1 + len(squares)),
    )(total, *squares)
    return out


def solution(mesh):
    placed = (
        P(("row", "col"), "fiber", None, None),
        P("fiber", None, "row", "col"),
        P("row", "fiber", None, None),
        P("row", "col"),
    )

    return jax.shard_map(
        local, mesh=mesh, in_specs=placed, out_specs=P(("row", "fiber"), "col"), check_vma=False
    )
```

profile of v0, /device:TPU:0, one launch (start us, length us, event | category | flops | bytes accessed | tf_op | source)
XLA Modules:
  0.0 106.9 jit_solution(1073596429343879326)
XLA Ops:
  0.0 3.1 %collective-permute-start.3 = (f32[1,2,96,1024]{3,2,1,0:T(8,128)}, f32[1,2,96,1024]{3,2,1,0:T(8,128)S(1)}, u32[]{:S(2)}, u32[]{:S(2)}) collective-permute-start(f32[1,2,96,1024]{3,2,1,0:T(8,128)} %refs_2_.1), channel_id=1, source_target_pairs={{0,8},{4,12},{8,24},{12,28},{24,16},{28,20},{16,0},{20,4},{1,9},{5... | collective-permute-start | bytes 2359304 | tf_op jit(solution)/shard_map/ppermute | solution.py:232
  5.0 2.4 %shard_map.46 = (f32[192,768]{1,0:T(8,128)S(1)}, f32[192,768]{1,0:T(8,128)S(1)}) custom-call(s32[3,1,2,6]{3,2,1,0:T(2,128)S(1)} %copy-done.3, f32[192,1,2,768]{3,2,1,0:T(2,128)S(1)} %copy-done), custom_call_target="tpu_custom_call" | custom-call | bytes 2359440 | tf_op jit(solution)/shard_map/pallas_call | solution.py:204
  12.0 11.7 %collective-permute-done.refs_1_ = f32[192,768]{1,0:T(8,128)S(1)} collective-permute-done((f32[192,768]{1,0:T(8,128)S(1)}, f32[192,768]{1,0:T(8,128)S(1)}, u32[]{:S(2)}, u32[]{:S(2)}) %collective-permute-start) | collective-permute-done | bytes 589856 | tf_op jit(solution)/shard_map/ppermute | solution.py:245
  23.7 12.4 %collective-permute-done.1.refs_2_ = f32[192,768]{1,0:T(8,128)S(1)} collective-permute-done((f32[192,768]{1,0:T(8,128)S(1)}, f32[192,768]{1,0:T(8,128)S(1)}, u32[]{:S(2)}, u32[]{:S(2)}) %collective-permute-start.1) | collective-permute-done | bytes 589856 | tf_op jit(solution)/shard_map/ppermute | solution.py:246
  36.9 3.7 %collective-permute-start.8 = (f32[1,2,96,256]{3,2,1,0:T(8,128)S(1)}, f32[1,2,96,256]{3,2,1,0:T(8,128)S(1)}, u32[]{:S(2)}, u32[]{:S(2)}) collective-permute-start(f32[1,2,96,256]{3,2,1,0:T(8,128)S(1)} %get-tuple-element.83), channel_id=1, source_target_pairs={{0,8},{4,12},{8,24},{12,28},{24,16},{28,20},{16,0},{20,4},{1,9},{5... | collective-permute-start | bytes 589832 | tf_op jit(solution)/shard_map/ppermute | solution.py:268
  42.1 2.6 %shard_map.49.near = f32[768,1024]{1,0:T(8,128)S(1)} custom-call(bf16[768,384]{1,0:T(8,128)(2,1)S(1)} %get-tuple-element.48.refs_0_, bf16[768,384]{1,0:T(8,128)(2,1)S(1)} %get-tuple-element.49.refs_1_, f32[1,2,96,1024]{3,2,1,0:T(8,128)S(1)} %collective-permute-done.3.refs_2_, f32[1,2,96,1024]{3,2,1,0:T(8,128)S(1)} %collective-permute-done.4.refs_3_, ...), custom_call_target="tpu_custom_call" | custom-call | flops 1811939328 | bytes 9043968 | tf_op jit(solution)/shard_map/pallas_call | solution.py:204
  45.2 3.3 %collective-permute-start.7 = (f32[1,2,96,256]{3,2,1,0:T(8,128)S(1)}, f32[1,2,96,256]{3,2,1,0:T(8,128)S(1)}, u32[]{:S(2)}, u32[]{:S(2)}) collective-permute-start(f32[1,2,96,256]{3,2,1,0:T(8,128)S(1)} %get-tuple-element.84), channel_id=1, source_target_pairs={{0,8},{4,12},{8,24},{12,28},{24,16},{28,20},{16,0},{20,4},{1,9},{5... | collective-permute-start | bytes 589832 | tf_op jit(solution)/shard_map/ppermute | solution.py:268
  48.6 5.1 %collective-permute-done.7.shard = f32[1,2,96,256]{3,2,1,0:T(8,128)S(1)} collective-permute-done((f32[1,2,96,256]{3,2,1,0:T(8,128)S(1)}, f32[1,2,96,256]{3,2,1,0:T(8,128)S(1)}, u32[]{:S(2)}, u32[]{:S(2)}) %collective-permute-start.7) | collective-permute-done | bytes 196640 | tf_op jit(solution)/shard_map/ppermute | solution.py:268
  54.3 2.2 %collective-permute-start.6 = (f32[1,2,96,256]{3,2,1,0:T(8,128)S(1)}, f32[1,2,96,256]{3,2,1,0:T(8,128)S(1)}, u32[]{:S(2)}, u32[]{:S(2)}) collective-permute-start(f32[1,2,96,256]{3,2,1,0:T(8,128)S(1)} %get-tuple-element.85), channel_id=1, source_target_pairs={{0,8},{4,12},{8,24},{12,28},{24,16},{28,20},{16,0},{20,4},{1,9},{5... | collective-permute-start | bytes 589832 | tf_op jit(solution)/shard_map/ppermute | solution.py:268
  56.6 6.2 %collective-permute-done.6.shard = f32[1,2,96,256]{3,2,1,0:T(8,128)S(1)} collective-permute-done((f32[1,2,96,256]{3,2,1,0:T(8,128)S(1)}, f32[1,2,96,256]{3,2,1,0:T(8,128)S(1)}, u32[]{:S(2)}, u32[]{:S(2)}) %collective-permute-start.6) | collective-permute-done | bytes 196640 | tf_op jit(solution)/shard_map/ppermute | solution.py:268
  63.3 2.0 %collective-permute-start.5 = (f32[1,2,96,256]{3,2,1,0:T(8,128)S(1)}, f32[1,2,96,256]{3,2,1,0:T(8,128)S(1)}, u32[]{:S(2)}, u32[]{:S(2)}) collective-permute-start(f32[1,2,96,256]{3,2,1,0:T(8,128)S(1)} %get-tuple-element.86), channel_id=1, source_target_pairs={{0,8},{4,12},{8,24},{12,28},{24,16},{28,20},{16,0},{20,4},{1,9},{5... | collective-permute-start | bytes 589832 | tf_op jit(solution)/shard_map/ppermute | solution.py:268
  65.3 6.2 %collective-permute-done.5.shard = f32[1,2,96,256]{3,2,1,0:T(8,128)S(1)} collective-permute-done((f32[1,2,96,256]{3,2,1,0:T(8,128)S(1)}, f32[1,2,96,256]{3,2,1,0:T(8,128)S(1)}, u32[]{:S(2)}, u32[]{:S(2)}) %collective-permute-start.5) | collective-permute-done | bytes 196640 | tf_op jit(solution)/shard_map/ppermute | solution.py:268
  72.1 1.8 %collective-permute-start.14 = (f32[192,256]{1,0:T(8,128)S(1)}, f32[192,256]{1,0:T(8,128)S(1)}, u32[]{:S(2)}, u32[]{:S(2)}) collective-permute-start(f32[192,256]{1,0:T(8,128)S(1)} %get-tuple-element.62), channel_id=1, source_target_pairs={{0,4},{4,0},{8,12},{12,8},{16,20},{20,16},{24,28},{28,24},{1,5},{5... | collective-permute-start | bytes 589832 | tf_op jit(solution)/shard_map/ppermute | solution.py:289
  74.2 1.7 %collective-permute-start.16 = (f32[192,256]{1,0:T(8,128)S(1)}, f32[192,256]{1,0:T(8,128)S(1)}, u32[]{:S(2)}, u32[]{:S(2)}) collective-permute-start(f32[192,256]{1,0:T(8,128)S(1)} %get-tuple-element.54), channel_id=1, source_target_pairs={{0,4},{4,0},{8,12},{12,8},{16,20},{20,16},{24,28},{28,24},{1,5},{5... | collective-permute-start | bytes 589832 | tf_op jit(solution)/shard_map/ppermute | solution.py:289
  76.3 3.6 %collective-permute-done.14.received = f32[192,256]{1,0:T(8,128)S(1)} collective-permute-done((f32[192,256]{1,0:T(8,128)S(1)}, f32[192,256]{1,0:T(8,128)S(1)}, u32[]{:S(2)}, u32[]{:S(2)}) %collective-permute-start.14) | collective-permute-done | bytes 196640 | tf_op jit(solution)/shard_map/ppermute | solution.py:289
  79.9 4.2 %collective-permute-done.15.received = f32[192,256]{1,0:T(8,128)S(1)} collective-permute-done((f32[192,256]{1,0:T(8,128)S(1)}, f32[192,256]{1,0:T(8,128)S(1)}, u32[]{:S(2)}, u32[]{:S(2)}) %collective-permute-start.15) | collective-permute-done | bytes 196640 | tf_op jit(solution)/shard_map/ppermute | solution.py:289
  84.1 4.2 %collective-permute-done.16.received = f32[192,256]{1,0:T(8,128)S(1)} collective-permute-done((f32[192,256]{1,0:T(8,128)S(1)}, f32[192,256]{1,0:T(8,128)S(1)}, u32[]{:S(2)}, u32[]{:S(2)}) %collective-permute-start.16) | collective-permute-done | bytes 196640 | tf_op jit(solution)/shard_map/ppermute | solution.py:289
  90.2 1.8 %collective-permute-done.13.received = f32[192,256]{1,0:T(8,128)S(1)} collective-permute-done((f32[192,256]{1,0:T(8,128)S(1)}, f32[192,256]{1,0:T(8,128)S(1)}, u32[]{:S(2)}, u32[]{:S(2)}) %collective-permute-start.13) | collective-permute-done | bytes 196640 | tf_op jit(solution)/shard_map/ppermute | solution.py:289
  93.9 1.7 %collective-permute-start.18 = (f32[1,1024]{1,0:T(1,128)S(1)}, f32[1,1024]{1,0:T(1,128)S(1)}, u32[]{:S(2)}, u32[]{:S(2)}) collective-permute-start(f32[1,1024]{1,0:T(1,128)S(1)} %add.12), channel_id=1, source_target_pairs={{0,4},{4,0},{8,12},{12,8},{16,20},{20,16},{24,28},{28,24},{1,5},{5... | collective-permute-start | bytes 12296 | tf_op jit(solution)/shard_map/ppermute | solution.py:47
  95.6 1.9 %collective-permute-done.18 = f32[1,1024]{1,0:T(1,128)S(1)} collective-permute-done((f32[1,1024]{1,0:T(1,128)S(1)}, f32[1,1024]{1,0:T(1,128)S(1)}, u32[]{:S(2)}, u32[]{:S(2)}) %collective-permute-start.18) | collective-permute-done | bytes 4128 | tf_op jit(solution)/shard_map/ppermute | solution.py:47
  97.5 1.9 %collective-permute-start.19 = (f32[1,1024]{1,0:T(1,128)S(1)}, f32[1,1024]{1,0:T(1,128)S(1)}, u32[]{:S(2)}, u32[]{:S(2)}) collective-permute-start(f32[1,1024]{1,0:T(1,128)S(1)} %add.13), channel_id=1, source_target_pairs={{0,8},{4,12},{8,0},{12,4},{16,24},{20,28},{24,16},{28,20},{1,9},{5... | collective-permute-start | bytes 12296 | tf_op jit(solution)/shard_map/ppermute | solution.py:47
  99.4 1.7 %collective-permute-done.19 = f32[1,1024]{1,0:T(1,128)S(1)} collective-permute-done((f32[1,1024]{1,0:T(1,128)S(1)}, f32[1,1024]{1,0:T(1,128)S(1)}, u32[]{:S(2)}, u32[]{:S(2)}) %collective-permute-start.19) | collective-permute-done | bytes 4128 | tf_op jit(solution)/shard_map/ppermute | solution.py:47
  101.1 3.3 %collective-permute-start.20 = (f32[1,1024]{1,0:T(1,128)S(1)}, f32[1,1024]{1,0:T(1,128)S(1)}, u32[]{:S(2)}, u32[]{:S(2)}) collective-permute-start(f32[1,1024]{1,0:T(1,128)S(1)} %add.14), channel_id=1, source_target_pairs={{0,16},{4,20},{8,24},{12,28},{16,0},{20,4},{24,8},{28,12},{1,17},{... | collective-permute-start | bytes 12296 | tf_op jit(solution)/shard_map/ppermute | solution.py:47
  104.4 1.6 %collective-permute-done.20 = f32[1,1024]{1,0:T(1,128)S(1)} collective-permute-done((f32[1,1024]{1,0:T(1,128)S(1)}, f32[1,1024]{1,0:T(1,128)S(1)}, u32[]{:S(2)}, u32[]{:S(2)}) %collective-permute-start.20) | collective-permute-done | bytes 4128 | tf_op jit(solution)/shard_map/ppermute | solution.py:47
  (48 shorter events, 16.5 us)
Async XLA Ops:
  0.0 36.9 %collective-permute-start.3 = (f32[1,2,96,1024]{3,2,1,0:T(8,128)}, f32[1,2,96,1024]{3,2,1,0:T(8,128)S(1)}, u32[]{:S(2)}, u32[]{:S(2)}) collective-permute-start(f32[1,2,96,1024]{3,2,1,0:T(8,128)} %refs_2_.1), channel_id=1, source_target_pairs={{0,8},{4,12},{8,24},{12,28},{24,16},{28,20},{16,0},{20,4},{1,9},{5... | collective-permute-start | bytes 2359304 | tf_op jit(solution)/shard_map/ppermute | solution.py:232
  3.1 1.3 %copy-start = (f32[192,1,2,768]{3,2,1,0:T(2,128)S(1)}, f32[192,1,2,768]{3,2,1,0:T(2,128)}, u32[]{:S(2)}) copy-start(f32[192,1,2,768]{3,2,1,0:T(2,128)} %source.1) | copy-start | bytes 3538948
  5.0 35.7 %copy-start.1 = (f32[1,2,96,1024]{3,2,1,0:T(8,128)S(1)}, f32[1,2,96,1024]{3,2,1,0:T(8,128)}, u32[]{:S(2)}) copy-start(f32[1,2,96,1024]{3,2,1,0:T(8,128)} %refs_2_.1) | copy-start | bytes 2359300
  7.4 16.3 %collective-permute-start = (f32[192,768]{1,0:T(8,128)S(1)}, f32[192,768]{1,0:T(8,128)S(1)}, u32[]{:S(2)}, u32[]{:S(2)}) collective-permute-start(f32[192,768]{1,0:T(8,128)S(1)} %get-tuple-element.44.refs_0_), channel_id=1, source_target_pairs={{0,2},{2,0},{1,3},{3,1},{4,6},{6,4},{5,7},{7,5},{8,10},{10,8},{9,1... | collective-permute-start | bytes 1769480 | tf_op jit(solution)/shard_map/ppermute | solution.py:245
  9.0 27.1 %collective-permute-start.1 = (f32[192,768]{1,0:T(8,128)S(1)}, f32[192,768]{1,0:T(8,128)S(1)}, u32[]{:S(2)}, u32[]{:S(2)}) collective-permute-start(f32[192,768]{1,0:T(8,128)S(1)} %get-tuple-element.45), channel_id=1, source_target_pairs={{0,4},{4,0},{8,12},{12,8},{16,20},{20,16},{24,28},{28,24},{1,5},{5... | collective-permute-start | bytes 1769480 | tf_op jit(solution)/shard_map/ppermute | solution.py:246
  10.5 25.6 %collective-permute-start.2 = (f32[192,768]{1,0:T(8,128)S(1)}, f32[192,768]{1,0:T(8,128)S(1)}, u32[]{:S(2)}, u32[]{:S(2)}) collective-permute-start(f32[192,768]{1,0:T(8,128)S(1)} %get-tuple-element.45), channel_id=1, source_target_pairs={{0,6},{2,4},{4,2},{6,0},{8,14},{10,12},{12,10},{14,8},{16,22},{18,... | collective-permute-start | bytes 1769480 | tf_op jit(solution)/shard_map/ppermute | solution.py:247
  11.0 31.1 %collective-permute-start.4 = (f32[1,2,96,1024]{3,2,1,0:T(8,128)}, f32[1,2,96,1024]{3,2,1,0:T(8,128)S(1)}, u32[]{:S(2)}, u32[]{:S(2)}) collective-permute-start(f32[1,2,96,1024]{3,2,1,0:T(8,128)} %refs_2_.1), channel_id=1, source_target_pairs={{0,16},{4,20},{8,0},{12,4},{24,8},{28,12},{16,24},{20,28},{1,17},{... | collective-permute-start | bytes 2359304 | tf_op jit(solution)/shard_map/ppermute | solution.py:233
  36.9 7.7 %collective-permute-start.8 = (f32[1,2,96,256]{3,2,1,0:T(8,128)S(1)}, f32[1,2,96,256]{3,2,1,0:T(8,128)S(1)}, u32[]{:S(2)}, u32[]{:S(2)}) collective-permute-start(f32[1,2,96,256]{3,2,1,0:T(8,128)S(1)} %get-tuple-element.83), channel_id=1, source_target_pairs={{0,8},{4,12},{8,24},{12,28},{24,16},{28,20},{16,0},{20,4},{1,9},{5... | collective-permute-start | bytes 589832 | tf_op jit(solution)/shard_map/ppermute | solution.py:268
  45.2 3.4 %collective-permute-start.9 = (f32[2,192,256]{2,1,0:T(8,128)S(1)}, f32[2,192,256]{2,1,0:T(8,128)S(1)}, u32[]{:S(2)}, u32[]{:S(2)}) collective-permute-start(f32[2,192,256]{2,1,0:T(8,128)S(1)} %get-tuple-element.53), channel_id=1, source_target_pairs={{0,1},{1,0},{2,3},{3,2},{4,5},{5,4},{6,7},{7,6},{8,9},{9,8},{10,11... | collective-permute-start | bytes 1179656 | tf_op jit(solution)/shard_map/ppermute | solution.py:286
  45.2 8.5 %collective-permute-start.7 = (f32[1,2,96,256]{3,2,1,0:T(8,128)S(1)}, f32[1,2,96,256]{3,2,1,0:T(8,128)S(1)}, u32[]{:S(2)}, u32[]{:S(2)}) collective-permute-start(f32[1,2,96,256]{3,2,1,0:T(8,128)S(1)} %get-tuple-element.84), channel_id=1, source_target_pairs={{0,8},{4,12},{8,24},{12,28},{24,16},{28,20},{16,0},{20,4},{1,9},{5... | collective-permute-start | bytes 589832 | tf_op jit(solution)/shard_map/ppermute | solution.py:268
  54.2 2.3 %collective-permute-start.10 = (f32[2,192,256]{2,1,0:T(8,128)S(1)}, f32[2,192,256]{2,1,0:T(8,128)S(1)}, u32[]{:S(2)}, u32[]{:S(2)}) collective-permute-start(f32[2,192,256]{2,1,0:T(8,128)S(1)} %get-tuple-element.57), channel_id=1, source_target_pairs={{0,1},{1,0},{2,3},{3,2},{4,5},{5,4},{6,7},{7,6},{8,9},{9,8},{10,11... | collective-permute-start | bytes 1179656 | tf_op jit(solution)/shard_map/ppermute | solution.py:286
  54.3 8.5 %collective-permute-start.6 = (f32[1,2,96,256]{3,2,1,0:T(8,128)S(1)}, f32[1,2,96,256]{3,2,1,0:T(8,128)S(1)}, u32[]{:S(2)}, u32[]{:S(2)}) collective-permute-start(f32[1,2,96,256]{3,2,1,0:T(8,128)S(1)} %get-tuple-element.85), channel_id=1, source_target_pairs={{0,8},{4,12},{8,24},{12,28},{24,16},{28,20},{16,0},{20,4},{1,9},{5... | collective-permute-start | bytes 589832 | tf_op jit(solution)/shard_map/ppermute | solution.py:268
  63.2 25.1 %copy-start.2 = (s32[3,8]{1,0:T(4,128)S(1)}, s32[3,8]{1,0:T(4,128)}, u32[]{:S(2)}) copy-start(s32[3,8]{1,0:T(4,128)} %pattern.9) | copy-start | bytes 292
  63.2 2.0 %collective-permute-start.11 = (f32[2,192,256]{2,1,0:T(8,128)S(1)}, f32[2,192,256]{2,1,0:T(8,128)S(1)}, u32[]{:S(2)}, u32[]{:S(2)}) collective-permute-start(f32[2,192,256]{2,1,0:T(8,128)S(1)} %get-tuple-element.61), channel_id=1, source_target_pairs={{0,1},{1,0},{2,3},{3,2},{4,5},{5,4},{6,7},{7,6},{8,9},{9,8},{10,11... | collective-permute-start | bytes 1179656 | tf_op jit(solution)/shard_map/ppermute | solution.py:286
  63.3 8.2 %collective-permute-start.5 = (f32[1,2,96,256]{3,2,1,0:T(8,128)S(1)}, f32[1,2,96,256]{3,2,1,0:T(8,128)S(1)}, u32[]{:S(2)}, u32[]{:S(2)}) collective-permute-start(f32[1,2,96,256]{3,2,1,0:T(8,128)S(1)} %get-tuple-element.86), channel_id=1, source_target_pairs={{0,8},{4,12},{8,24},{12,28},{24,16},{28,20},{16,0},{20,4},{1,9},{5... | collective-permute-start | bytes 589832 | tf_op jit(solution)/shard_map/ppermute | solution.py:268
  72.0 3.9 %collective-permute-start.12 = (f32[2,192,256]{2,1,0:T(8,128)S(1)}, f32[2,192,256]{2,1,0:T(8,128)S(1)}, u32[]{:S(2)}, u32[]{:S(2)}) collective-permute-start(f32[2,192,256]{2,1,0:T(8,128)S(1)} %get-tuple-element.65), channel_id=1, source_target_pairs={{0,1},{1,0},{2,3},{3,2},{4,5},{5,4},{6,7},{7,6},{8,9},{9,8},{10,11... | collective-permute-start | bytes 1179656 | tf_op jit(solution)/shard_map/ppermute | solution.py:286
  72.1 7.8 %collective-permute-start.14 = (f32[192,256]{1,0:T(8,128)S(1)}, f32[192,256]{1,0:T(8,128)S(1)}, u32[]{:S(2)}, u32[]{:S(2)}) collective-permute-start(f32[192,256]{1,0:T(8,128)S(1)} %get-tuple-element.62), channel_id=1, source_target_pairs={{0,4},{4,0},{8,12},{12,8},{16,20},{20,16},{24,28},{28,24},{1,5},{5... | collective-permute-start | bytes 589832 | tf_op jit(solution)/shard_map/ppermute | solution.py:289
  73.8 10.3 %collective-permute-start.15 = (f32[192,256]{1,0:T(8,128)S(1)}, f32[192,256]{1,0:T(8,128)S(1)}, u32[]{:S(2)}, u32[]{:S(2)}) collective-permute-start(f32[192,256]{1,0:T(8,128)S(1)} %get-tuple-element.58), channel_id=1, source_target_pairs={{0,4},{4,0},{8,12},{12,8},{16,20},{20,16},{24,28},{28,24},{1,5},{5... | collective-permute-start | bytes 589832 | tf_op jit(solution)/shard_map/ppermute | solution.py:289
  74.2 14.2 %collective-permute-start.16 = (f32[192,256]{1,0:T(8,128)S(1)}, f32[192,256]{1,0:T(8,128)S(1)}, u32[]{:S(2)}, u32[]{:S(2)}) collective-permute-start(f32[192,256]{1,0:T(8,128)S(1)} %get-tuple-element.54), channel_id=1, source_target_pairs={{0,4},{4,0},{8,12},{12,8},{16,20},{20,16},{24,28},{28,24},{1,5},{5... | collective-permute-start | bytes 589832 | tf_op jit(solution)/shard_map/ppermute | solution.py:289
  75.9 16.1 %collective-permute-start.13 = (f32[192,256]{1,0:T(8,128)S(1)}, f32[192,256]{1,0:T(8,128)S(1)}, u32[]{:S(2)}, u32[]{:S(2)}) collective-permute-start(f32[192,256]{1,0:T(8,128)S(1)} %get-tuple-element.67), channel_id=1, source_target_pairs={{0,4},{4,0},{8,12},{12,8},{16,20},{20,16},{24,28},{28,24},{1,5},{5... | collective-permute-start | bytes 589832 | tf_op jit(solution)/shard_map/ppermute | solution.py:289
  92.6 1.2 %collective-permute-start.17 = (f32[1,1024]{1,0:T(1,128)S(1)}, f32[1,1024]{1,0:T(1,128)S(1)}, u32[]{:S(2)}, u32[]{:S(2)}) collective-permute-start(f32[1,1024]{1,0:T(1,128)S(1)} %get-tuple-element.78), channel_id=1, source_target_pairs={{0,1},{1,0},{2,3},{3,2},{4,5},{5,4},{6,7},{7,6},{8,9},{9,8},{10,11... | collective-permute-start | bytes 12296 | tf_op jit(solution)/shard_map/ppermute | solution.py:47
  93.9 3.6 %collective-permute-start.18 = (f32[1,1024]{1,0:T(1,128)S(1)}, f32[1,1024]{1,0:T(1,128)S(1)}, u32[]{:S(2)}, u32[]{:S(2)}) collective-permute-start(f32[1,1024]{1,0:T(1,128)S(1)} %add.12), channel_id=1, source_target_pairs={{0,4},{4,0},{8,12},{12,8},{16,20},{20,16},{24,28},{28,24},{1,5},{5... | collective-permute-start | bytes 12296 | tf_op jit(solution)/shard_map/ppermute | solution.py:47
  97.5 3.6 %collective-permute-start.19 = (f32[1,1024]{1,0:T(1,128)S(1)}, f32[1,1024]{1,0:T(1,128)S(1)}, u32[]{:S(2)}, u32[]{:S(2)}) collective-permute-start(f32[1,1024]{1,0:T(1,128)S(1)} %add.13), channel_id=1, source_target_pairs={{0,8},{4,12},{8,0},{12,4},{16,24},{20,28},{24,16},{28,20},{1,9},{5... | collective-permute-start | bytes 12296 | tf_op jit(solution)/shard_map/ppermute | solution.py:47
  101.1 4.8 %collective-permute-start.20 = (f32[1,1024]{1,0:T(1,128)S(1)}, f32[1,1024]{1,0:T(1,128)S(1)}, u32[]{:S(2)}, u32[]{:S(2)}) collective-permute-start(f32[1,1024]{1,0:T(1,128)S(1)} %add.14), channel_id=1, source_target_pairs={{0,16},{4,20},{8,24},{12,28},{16,0},{20,4},{24,8},{28,12},{1,17},{... | collective-permute-start | bytes 12296 | tf_op jit(solution)/shard_map/ppermute | solution.py:47
  (1 other events, 0.7 us)
where the time goes:
time: 107 us
  waiting for transfers between devices  61.8 us (58%)
  starting transfers between devices  30.3 us (28%)
  Pallas kernels  12.6 us (12%)
  local copies, waits for them, and re-layouts  2.03 us (2%)
    ppermute x4, waiting for transfers between devices, local(): lax.ppermute(down[..., j * CHUNK:(j + 1) * CHUNK], 'row', line_pairs(1))  17.5 us
    ppermute x4, waiting for transfers between devices, local(): far[j] = (stays, lax.ppermute(goes, 'row', swap_y))  13.8 us
    pallas_call x17, Pallas kernels, run(): pl.pallas_call(kernel, out_shape=out_shapes, in_specs=specs, out_specs=[V...  12.6 us
    ppermute x1, waiting for transfers between devices, local(): from_y = lax.ppermute(other, 'row', swap_y)  12.4 us
    ppermute x1, waiting for transfers between devices, local(): from_x = lax.ppermute(mine, 'col', swap)  11.7 us
    ppermute x4, starting transfers between devices, local(): lax.ppermute(down[..., j * CHUNK:(j + 1) * CHUNK], 'row', line_pairs(1))  11.3 us
    ppermute x4, starting transfers between devices, all_sum(): total = total + lax.ppermute(value, axis_name, pairs)  6.92 us
    ppermute x4, waiting for transfers between devices, all_sum(): total = total + lax.ppermute(value, axis_name, pairs)  6.36 us
  transfers between devices with their start and end apart: 21, of which 13 were waited for; matrix products, arithmetic and copies ran while one was open for 0% of the time, Pallas kernels for 9%

commit v1 on v0

--- a/solution.py
+++ b/solution.py
@@ -12,8 +12,7 @@
 
 
 EPS = 1e-06
-TILE = 256
-CHUNK = 256
+CHUNKS = (128, 256, 256, 256, 128)
 
 
 LINE = (0, 1, 3, 2)
@@ -93,27 +92,23 @@
     return dot(a_high, b_high) + (dot(a_high, b_low) + dot(a_low, b_high))
 
 
-def left_kernel(steps, pattern, source, mine, other, turned):
-    rows, _, sections, width = source.shape
+def left_kernel(steps, rows, pattern, source, mine, other, turned):
+    group, _, sections, width = source.shape
     n_row, row = lax.axis_size("row"), lax.axis_index("row")
     depth = width // n_row
-    group = 64
-    for g in range(rows // group):
-        part = pl.ds(g * group, group)
-        block_row = (lax.axis_index("col") * rows + g * group) // BLK
-        for s in range(sections):
-            kept = []
-            for w in range(width // BLK):
-                keep = pattern[block_row, 0, s, w]
-                piece = source[part, 0, s, pl.ds(w * BLK, BLK)]
-                kept.append(jnp.where(keep != 0, piece, 0.0))
-            value = jnp.concatenate(kept, axis=1)
-            for r in range(n_row):
-                turned[r, s, part, :] = value[:, r * depth : (r + 1) * depth]
-        for out, parity in ((mine, row % 2), (other, 1 - row % 2)):
-            owners = [line_at(row // 2, step) * 2 + parity for step in steps]
-            pieces = [turned[r, s, part, :] for r in owners for s in range(sections)]
-            out[part, :] = jnp.concatenate(pieces, axis=1)
+    block_row = (lax.axis_index("col") * rows + pl.program_id(0) * group) // BLK
+    for s in range(sections):
+        kept = []
+        for w in range(width // BLK):
+            keep = pattern[block_row, 0, s, w]
+            kept.append(jnp.where(keep != 0, source[:, 0, s, pl.ds(w * BLK, BLK)], 0.0))
+        value = jnp.concatenate(kept, axis=1)
+        for r in range(n_row):
+            turned[r, s] = value[:, r * depth : (r + 1) * depth]
+    for out, parity in ((mine, row % 2), (other, 1 - row % 2)):
+        owners = [line_at(row // 2, step) * 2 + parity for step in steps]
+        pieces = [turned[r, s] for r in owners for s in range(sections)]
+        out[...] = jnp.concatenate(pieces, axis=1)
 
 
 def order_kernel(cuts, *refs):
@@ -129,21 +124,20 @@
             outs[2 * i + 1][pl.ds(start, rows), :] = low
 
 
-def group_kernel(count, *refs):
-    high, low, *rest = refs
-    shards, (*near, out, b_high, b_low) = rest[:count], rest[count:]
-    _, sections, depth, columns = shards[0].shape
-    for i in range(count * sections):
-        part = pl.ds(i * depth, depth)
-        b_high[part, :], b_low[part, :] = split(shards[i // sections][0, i % sections])
-    for t in range(columns // TILE):
-        tile = pl.ds(t * TILE, TILE)
-        total = product3(high[...], low[...], b_high[:, tile], b_low[:, tile])
-        out[:, tile] = near[0][:, tile] + total if near else total
-
-
-def far_kernel(first, high, low, near, shard, kept, sent, b_high, b_low):
-    _, sections, depth, columns = shard.shape
+def near_kernel(first, own_high, own_low, high, low, own, down, up, out, b_high, b_low):
+    _, sections, depth, _ = own.shape
+    tile = slice(first, first + out.shape[1])
+    for i, shard in enumerate((down, up, own)):
+        for s in range(sections):
+            part = pl.ds((i * sections + s) * depth, depth)
+            b_high[part, :], b_low[part, :] = split(shard[0, s, :, tile])
+    cut = 2 * sections * depth
+    total = product3(high[...], low[...], b_high[:cut, :], b_low[:cut, :])
+    out[...] = total + product3(own_high[...], own_low[...], b_high[cut:, :], b_low[cut:, :])
+
+
+def far_kernel(high, low, near, shard, kept, sent, b_high, b_low):
+    _, sections, depth, _ = shard.shape
     rows = kept.shape[1]
     for s in range(sections):
         part = pl.ds(s * depth, depth)
@@ -152,7 +146,7 @@
     for q in range(4):
         out = sent if q >= 2 else kept
         block = pl.ds(q * rows, rows)
-        out[q % 2] = near[block, first : first + columns] + value[q * rows : (q + 1) * rows]
+        out[q % 2] = near[block, :] + value[q * rows : (q + 1) * rows]
 
 
 def fold_kernel(kept, received, mine, other):
@@ -178,7 +172,7 @@
             total += jnp.sum(value.reshape(group // 8, 8, BLK), axis=0)
         sums[:, pl.ds(first + w * BLK, BLK)] = jnp.sum(total, axis=0, keepdims=True)
     for old in before:
-        sums[:, pl.ds(0, first)] = old[...]
+        sums[:, :first] = old[...]
 
 
 def scale_kernel(row_total, sums, *refs):
@@ -198,17 +192,17 @@
 SMEM = pl.BlockSpec(memory_space=pltpu.SMEM)
 
 
-def call(kernel, out_shapes, specs, scratch=(), flops=0):
+def call(kernel, out_shapes, specs, scratch=(), flops=0, limit=16, **kwargs):
     def run(*args):
         moved = sum(a.size * a.dtype.itemsize for a in (*args, *out_shapes))
         return pl.pallas_call(
             kernel,
             out_shape=out_shapes,
             in_specs=specs,
-            out_specs=[VMEM] * len(out_shapes),
             scratch_shapes=scratch,
             cost_estimate=pl.CostEstimate(flops=flops, bytes_accessed=moved, transcendentals=0),
-            compiler_params=pltpu.CompilerParams(vmem_limit_bytes=16 * 2**20),
+            compiler_params=pltpu.CompilerParams(vmem_limit_bytes=limit * 2**20),
+            **{"out_specs": [VMEM] * len(out_shapes), **kwargs},
         )(*args)
 
     return run
@@ -220,7 +214,7 @@
     n_row, n_col, fibers = (lax.axis_size(name) for name in ("row", "col", "fiber"))
     local_rows = rows * n_col
     share = local_rows // fibers
-    if (n_row, n_col, fibers, sections) != (8, 2, 2, 2):
+    if (n_row, n_col, fibers, sections, columns) != (8, 2, 2, 2, sum(CHUNKS)):
         return gathered(a_panels, b_panels, a_pattern, c_pattern)
 
     f32, bf16 = jnp.float32, jnp.bfloat16
@@ -233,11 +227,16 @@
     up = lax.ppermute(b_panels, "row", line_pairs(-1))
 
     steps = (-1, 1, 0, 2)
+    group = 64
+    blocked = pl.BlockSpec((group, half), lambda i: (i, 0))
     mine, other = call(
-        functools.partial(left_kernel, steps),
+        functools.partial(left_kernel, steps, rows),
         [shape((rows, half), f32)] * 2,
-        [SMEM, VMEM],
-        [pltpu.VMEM((n_row, sections, rows, depth), f32)],
+        [SMEM, pl.BlockSpec((group, 1, sections, width), lambda i: (i, 0, 0, 0))],
+        [pltpu.VMEM((n_row, sections, group, depth), f32)],
+        limit=56,
+        grid=(rows // group,),
+        out_specs=[blocked] * 2,
     )(a_pattern, a_panels)
     swap = [(0, 1), (1, 0)]
     swap_y = [(r, r ^ 1) for r in range(n_row)]
@@ -252,47 +251,49 @@
         [VMEM] * 4,
     )(mine, from_x, from_y, from_both)
 
-    def product(high, low, *shards_and_near):
-        depth_here = high.shape[1]
-        factor = pltpu.VMEM((depth_here, columns), bf16)
+    starts = [sum(CHUNKS[:j]) for j in range(len(CHUNKS))]
+    far = [
+        lax.ppermute(down[..., first : first + chunk], "row", line_pairs(1))
+        for first, chunk in zip(starts, CHUNKS, strict=True)
+    ]
+
+    def near_product(j):
+        factor = pltpu.VMEM((3 * shard_depth, CHUNKS[j]), bf16)
         (total,) = call(
-            functools.partial(group_kernel, depth_here // shard_depth),
-            [shape((plane_rows, columns), f32)],
-            [VMEM] * (2 + len(shards_and_near)),
+            functools.partial(near_kernel, starts[j]),
+            [shape((plane_rows, CHUNKS[j]), f32)],
+            [VMEM] * 7,
             [factor, factor],
-            6 * plane_rows * columns * depth_here,
-        )(high, low, *shards_and_near)
+            6 * plane_rows * CHUNKS[j] * 3 * shard_depth,
+        )(own_high, own_low, near_high, near_low, b_panels, down, up)
         return total
 
-    far = [
-        lax.ppermute(down[..., j * CHUNK : (j + 1) * CHUNK], "row", line_pairs(1))
-        for j in range(columns // CHUNK)
-    ]
-    near = product(own_high, own_low, b_panels)
-    near = product(near_high, near_low, down, up, near)
-
     ends = []
-    for j, shard in enumerate(far):
+    near = near_product(0)
+    for j, (shard, chunk) in enumerate(zip(far, CHUNKS, strict=True)):
         if ends:
             shard, _ = together(shard, ends[-1])
-        factor = pltpu.VMEM((shard_depth, CHUNK), bf16)
+        factor = pltpu.VMEM((shard_depth, chunk), bf16)
         kept, sent = call(
-            functools.partial(far_kernel, j * CHUNK),
-            [shape((2, rows, CHUNK), f32)] * 2,
+            far_kernel,
+            [shape((2, rows, chunk), f32)] * 2,
             [VMEM] * 4,
             [factor, factor],
-            6 * plane_rows * CHUNK * shard_depth,
+            6 * plane_rows * chunk * shard_depth,
         )(far_high, far_low, near, shard)
         received = lax.ppermute(sent, "fiber", swap)
-        stays, goes = call(fold_kernel, [shape((rows, CHUNK), f32)] * 2, [VMEM] * 2)(kept, received)
+        if j + 1 < len(CHUNKS):
+            near = near_product(j + 1)
+            received, near = together(received, near)
+        stays, goes = call(fold_kernel, [shape((rows, chunk), f32)] * 2, [VMEM] * 2)(kept, received)
         ends.append(goes)
         far[j] = stays, lax.ppermute(goes, "row", swap_y)
     squares, sums = [], []
     for j, (stays, received) in enumerate(far):
         received, _ = together(received, ends[-1])
         square, total = call(
-            functools.partial(square_kernel, j * CHUNK),
-            [shape((rows, CHUNK), f32), shape((1, (j + 1) * CHUNK), f32)],
+            functools.partial(square_kernel, starts[j]),
+            [shape((rows, CHUNKS[j]), f32), shape((1, starts[j] + CHUNKS[j]), f32)],
             [SMEM] + [VMEM] * (2 + len(sums)),
         )(c_pattern, stays, received, *sums)
         squares.append(square)
@@ -314,6 +315,4 @@
         P("row", "col"),
     )
 
-    return jax.shard_map(
-        local, mesh=mesh, in_specs=placed, out_specs=P(("row", "fiber"), "col"), check_vma=False
-    )
+    return jax.shard_map(local, mesh=mesh, in_specs=placed, out_specs=P(("row", "fiber"), "col"), check_vma=False)

time: 107 us -> 114 us (1.065)
  starting transfers between devices: 30.3 us -> 48.7 us
  waiting for transfers between devices: 61.8 us -> 46.9 us
  Pallas kernels: 12.6 us -> 16.6 us
    ppermute x4 -> x5, starting transfers between devices: 11.3 us -> 28.3 us  [local(): lax.ppermute(down[..., first:first + chunk], 'row', line_pairs(1))]
    ppermute x1, waiting for transfers between devices: 12.4 us -> 0.01 us  [local(): from_y = lax.ppermute(other, 'row', swap_y)]
    ppermute x1, waiting for transfers between devices: 11.7 us -> 0.01 us  [local(): from_x = lax.ppermute(mine, 'col', swap)]
    ppermute x1, waiting for transfers between devices: 0.01 us -> 10.1 us  [local(): down = lax.ppermute(b_panels, 'row', line_pairs(1))]
    pallas_call x17 -> x23, Pallas kernels: 12.6 us -> 16.6 us  [run(): pl.pallas_call(kernel, out_shape=out_shapes, in_specs=specs, scratch_shap...]
    ppermute x4 -> x5, starting transfers between devices: 4.18 us -> 5.7 us  [local(): far[j] = (stays, lax.ppermute(goes, 'row', swap_y))]
    ppermute x4 -> x5, waiting for transfers between devices: 13.8 us -> 12.6 us  [local(): far[j] = (stays, lax.ppermute(goes, 'row', swap_y))]
    ppermute x4 -> x5, waiting for transfers between devices: 17.5 us -> 17.6 us  [local(): lax.ppermute(down[..., first:first + chunk], 'row', line_pairs(1))]
  transfers between devices with their start and end apart: 21 -> 24, of which waited for: 13 -> 13; matrix products, arithmetic and copies ran while one was open for 0% -> 0% of each run, Pallas kernels for 9% -> 11%
where the time goes in v1:
time: 114 us
  starting transfers between devices  48.7 us (43%)
  waiting for transfers between devices  46.9 us (41%)
  Pallas kernels  16.6 us (15%)
    ppermute x5, starting transfers between devices, local(): lax.ppermute(down[..., first:first + chunk], 'row', line_pairs(1))  28.3 us
    ppermute x5, waiting for transfers between devices, local(): lax.ppermute(down[..., first:first + chunk], 'row', line_pairs(1))  17.6 us
    pallas_call x23, Pallas kernels, run(): pl.pallas_call(kernel, out_shape=out_shapes, in_specs=specs, scratch_shap...  16.6 us
    ppermute x5, waiting for transfers between devices, local(): far[j] = (stays, lax.ppermute(goes, 'row', swap_y))  12.6 us
    ppermute x1, waiting for transfers between devices, local(): down = lax.ppermute(b_panels, 'row', line_pairs(1))  10.1 us
    ppermute x4, starting transfers between devices, all_sum(): total = total + lax.ppermute(value, axis_name, pairs)  6.75 us
    ppermute x4, waiting for transfers between devices, all_sum(): total = total + lax.ppermute(value, axis_name, pairs)  6.53 us
    ppermute x5, starting transfers between devices, local(): far[j] = (stays, lax.ppermute(goes, 'row', swap_y))  5.7 us
  transfers between devices with their start and end apart: 24, of which 13 were waited for; matrix products, arithmetic and copies ran while one was open for 0% of the time, Pallas kernels for 11%

profile of v1, /device:TPU:0, one launch (start us, length us, event | category | flops | bytes accessed | tf_op | source)
XLA Modules:
  0.0 113.7 jit_solution(7981641253773127794)
XLA Ops:
  0.0 3.1 %collective-permute-start.3 = (f32[1,2,96,1024]{3,2,1,0:T(8,128)}, f32[1,2,96,1024]{3,2,1,0:T(8,128)S(1)}, u32[]{:S(2)}, u32[]{:S(2)}) collective-permute-start(f32[1,2,96,1024]{3,2,1,0:T(8,128)} %own.9), channel_id=1, source_target_pairs={{0,8},{4,12},{8,24},{12,28},{24,16},{28,20},{16,0},{20,4},{1,9},{5... | collective-permute-start | bytes 2359304 | tf_op jit(solution)/shard_map/ppermute | solution.py:226
  4.1 4.2 %shard_map.46 = (f32[192,768]{1,0:T(8,128)}, f32[192,768]{1,0:T(8,128)}) custom-call(s32[3,1,2,6]{3,2,1,0:T(2,128)} %pattern.6, f32[192,1,2,768]{3,2,1,0:T(2,128)} %source.1), custom_call_target="tpu_custom_call" | custom-call | bytes 2359440 | tf_op jit(solution)/shard_map/pallas_call | solution.py:198
  8.3 1.8 %collective-permute-start = (f32[192,768]{1,0:T(8,128)}, f32[192,768]{1,0:T(8,128)S(1)}, u32[]{:S(2)}, u32[]{:S(2)}) collective-permute-start(f32[192,768]{1,0:T(8,128)} %get-tuple-element.60.refs_0_), channel_id=1, source_target_pairs={{0,2},{2,0},{1,3},{3,1},{4,6},{6,4},{5,7},{7,5},{8,10},{10,8},{9,1... | collective-permute-start | bytes 1769480 | tf_op jit(solution)/shard_map/ppermute | solution.py:244
  11.8 10.1 %collective-permute-done.3.down = f32[1,2,96,1024]{3,2,1,0:T(8,128)S(1)} collective-permute-done((f32[1,2,96,1024]{3,2,1,0:T(8,128)}, f32[1,2,96,1024]{3,2,1,0:T(8,128)S(1)}, u32[]{:S(2)}, u32[]{:S(2)}) %collective-permute-start.3) | collective-permute-done | bytes 786464 | tf_op jit(solution)/shard_map/ppermute | solution.py:226
  21.9 18.8 %collective-permute-start.5 = (f32[1,2,96,128]{3,2,1,0:T(8,128)S(1)}, f32[1,2,96,128]{3,2,1,0:T(8,128)S(1)}, u32[]{:S(2)}, u32[]{:S(2)}) collective-permute-start(f32[1,2,96,128]{3,2,1,0:T(8,128)S(1)} %get-tuple-element.116), channel_id=1, source_target_pairs={{0,8},{4,12},{8,24},{12,28},{24,16},{28,20},{16,0},{20,4},{1,9},{5... | collective-permute-start | bytes 294920 | tf_op jit(solution)/shard_map/ppermute | solution.py:256
  44.2 3.3 %collective-permute-start.7 = (f32[1,2,96,256]{3,2,1,0:T(8,128)S(1)}, f32[1,2,96,256]{3,2,1,0:T(8,128)S(1)}, u32[]{:S(2)}, u32[]{:S(2)}) collective-permute-start(f32[1,2,96,256]{3,2,1,0:T(8,128)S(1)} %get-tuple-element.119), channel_id=1, source_target_pairs={{0,8},{4,12},{8,24},{12,28},{24,16},{28,20},{16,0},{20,4},{1,9},{5... | collective-permute-start | bytes 589832 | tf_op jit(solution)/shard_map/ppermute | solution.py:256
  48.7 4.2 %collective-permute-done.7.shard = f32[1,2,96,256]{3,2,1,0:T(8,128)S(1)} collective-permute-done((f32[1,2,96,256]{3,2,1,0:T(8,128)S(1)}, f32[1,2,96,256]{3,2,1,0:T(8,128)S(1)}, u32[]{:S(2)}, u32[]{:S(2)}) %collective-permute-start.7) | collective-permute-done | bytes 196640 | tf_op jit(solution)/shard_map/ppermute | solution.py:256
  53.4 2.2 %collective-permute-start.9 = (f32[1,2,96,256]{3,2,1,0:T(8,128)S(1)}, f32[1,2,96,256]{3,2,1,0:T(8,128)S(1)}, u32[]{:S(2)}, u32[]{:S(2)}) collective-permute-start(f32[1,2,96,256]{3,2,1,0:T(8,128)S(1)} %get-tuple-element.118), channel_id=1, source_target_pairs={{0,8},{4,12},{8,24},{12,28},{24,16},{28,20},{16,0},{20,4},{1,9},{5... | collective-permute-start | bytes 589832 | tf_op jit(solution)/shard_map/ppermute | solution.py:256
  56.8 5.1 %collective-permute-done.9.shard = f32[1,2,96,256]{3,2,1,0:T(8,128)S(1)} collective-permute-done((f32[1,2,96,256]{3,2,1,0:T(8,128)S(1)}, f32[1,2,96,256]{3,2,1,0:T(8,128)S(1)}, u32[]{:S(2)}, u32[]{:S(2)}) %collective-permute-start.9) | collective-permute-done | bytes 196640 | tf_op jit(solution)/shard_map/ppermute | solution.py:256
  62.5 2.0 %collective-permute-start.11 = (f32[1,2,96,256]{3,2,1,0:T(8,128)S(1)}, f32[1,2,96,256]{3,2,1,0:T(8,128)S(1)}, u32[]{:S(2)}, u32[]{:S(2)}) collective-permute-start(f32[1,2,96,256]{3,2,1,0:T(8,128)S(1)} %get-tuple-element.117), channel_id=1, source_target_pairs={{0,8},{4,12},{8,24},{12,28},{24,16},{28,20},{16,0},{20,4},{1,9},{5... | collective-permute-start | bytes 589832 | tf_op jit(solution)/shard_map/ppermute | solution.py:256
  65.6 5.1 %collective-permute-done.11.shard = f32[1,2,96,256]{3,2,1,0:T(8,128)S(1)} collective-permute-done((f32[1,2,96,256]{3,2,1,0:T(8,128)S(1)}, f32[1,2,96,256]{3,2,1,0:T(8,128)S(1)}, u32[]{:S(2)}, u32[]{:S(2)}) %collective-permute-start.11) | collective-permute-done | bytes 196640 | tf_op jit(solution)/shard_map/ppermute | solution.py:256
  71.2 2.0 %collective-permute-start.13 = (f32[1,2,96,128]{3,2,1,0:T(8,128)S(1)}, f32[1,2,96,128]{3,2,1,0:T(8,128)S(1)}, u32[]{:S(2)}, u32[]{:S(2)}) collective-permute-start(f32[1,2,96,128]{3,2,1,0:T(8,128)S(1)} %get-tuple-element.115), channel_id=1, source_target_pairs={{0,8},{4,12},{8,24},{12,28},{24,16},{28,20},{16,0},{20,4},{1,9},{5... | collective-permute-start | bytes 294920 | tf_op jit(solution)/shard_map/ppermute | solution.py:256
  74.2 3.1 %collective-permute-done.13.shard = f32[1,2,96,128]{3,2,1,0:T(8,128)S(1)} collective-permute-done((f32[1,2,96,128]{3,2,1,0:T(8,128)S(1)}, f32[1,2,96,128]{3,2,1,0:T(8,128)S(1)}, u32[]{:S(2)}, u32[]{:S(2)}) %collective-permute-start.13) | collective-permute-done | bytes 98336 | tf_op jit(solution)/shard_map/ppermute | solution.py:256
  77.9 1.6 %collective-permute-start.16 = (f32[192,256]{1,0:T(8,128)S(1)}, f32[192,256]{1,0:T(8,128)S(1)}, u32[]{:S(2)}, u32[]{:S(2)}) collective-permute-start(f32[192,256]{1,0:T(8,128)S(1)} %get-tuple-element.90), channel_id=1, source_target_pairs={{0,4},{4,0},{8,12},{12,8},{16,20},{20,16},{24,28},{28,24},{1,5},{5... | collective-permute-start | bytes 589832 | tf_op jit(solution)/shard_map/ppermute | solution.py:290
  82.0 1.6 %collective-permute-start.15 = (f32[192,128]{1,0:T(8,128)S(1)}, f32[192,128]{1,0:T(8,128)S(1)}, u32[]{:S(2)}, u32[]{:S(2)}) collective-permute-start(f32[192,128]{1,0:T(8,128)S(1)} %get-tuple-element.95), channel_id=1, source_target_pairs={{0,4},{4,0},{8,12},{12,8},{16,20},{20,16},{24,28},{28,24},{1,5},{5... | collective-permute-start | bytes 294920 | tf_op jit(solution)/shard_map/ppermute | solution.py:290
  83.6 2.1 %collective-permute-done.16.received = f32[192,256]{1,0:T(8,128)S(1)} collective-permute-done((f32[192,256]{1,0:T(8,128)S(1)}, f32[192,256]{1,0:T(8,128)S(1)}, u32[]{:S(2)}, u32[]{:S(2)}) %collective-permute-start.16) | collective-permute-done | bytes 196640 | tf_op jit(solution)/shard_map/ppermute | solution.py:290
  85.7 4.2 %collective-permute-done.17.received = f32[192,256]{1,0:T(8,128)S(1)} collective-permute-done((f32[192,256]{1,0:T(8,128)S(1)}, f32[192,256]{1,0:T(8,128)S(1)}, u32[]{:S(2)}, u32[]{:S(2)}) %collective-permute-start.17) | collective-permute-done | bytes 196640 | tf_op jit(solution)/shard_map/ppermute | solution.py:290
  89.9 4.2 %collective-permute-done.18.received = f32[192,256]{1,0:T(8,128)S(1)} collective-permute-done((f32[192,256]{1,0:T(8,128)S(1)}, f32[192,256]{1,0:T(8,128)S(1)}, u32[]{:S(2)}, u32[]{:S(2)}) %collective-permute-start.18) | collective-permute-done | bytes 196640 | tf_op jit(solution)/shard_map/ppermute | solution.py:290
  94.1 2.1 %collective-permute-done.19.received = f32[192,128]{1,0:T(8,128)S(1)} collective-permute-done((f32[192,128]{1,0:T(8,128)S(1)}, f32[192,128]{1,0:T(8,128)S(1)}, u32[]{:S(2)}, u32[]{:S(2)}) %collective-permute-start.19) | collective-permute-done | bytes 98336 | tf_op jit(solution)/shard_map/ppermute | solution.py:290
  102.1 2.1 %collective-permute-done.21 = f32[1,1024]{1,0:T(1,128)S(1)} collective-permute-done((f32[1,1024]{1,0:T(1,128)S(1)}, f32[1,1024]{1,0:T(1,128)S(1)}, u32[]{:S(2)}, u32[]{:S(2)}) %collective-permute-start.21) | collective-permute-done | bytes 4128 | tf_op jit(solution)/shard_map/ppermute | solution.py:46
  104.2 1.9 %collective-permute-start.22 = (f32[1,1024]{1,0:T(1,128)S(1)}, f32[1,1024]{1,0:T(1,128)S(1)}, u32[]{:S(2)}, u32[]{:S(2)}) collective-permute-start(f32[1,1024]{1,0:T(1,128)S(1)} %add.13), channel_id=1, source_target_pairs={{0,8},{4,12},{8,0},{12,4},{16,24},{20,28},{24,16},{28,20},{1,9},{5... | collective-permute-start | bytes 12296 | tf_op jit(solution)/shard_map/ppermute | solution.py:46
  106.1 1.7 %collective-permute-done.22 = f32[1,1024]{1,0:T(1,128)S(1)} collective-permute-done((f32[1,1024]{1,0:T(1,128)S(1)}, f32[1,1024]{1,0:T(1,128)S(1)}, u32[]{:S(2)}, u32[]{:S(2)}) %collective-permute-start.22) | collective-permute-done | bytes 4128 | tf_op jit(solution)/shard_map/ppermute | solution.py:46
  107.9 3.3 %collective-permute-start.23 = (f32[1,1024]{1,0:T(1,128)S(1)}, f32[1,1024]{1,0:T(1,128)S(1)}, u32[]{:S(2)}, u32[]{:S(2)}) collective-permute-start(f32[1,1024]{1,0:T(1,128)S(1)} %add.14), channel_id=1, source_target_pairs={{0,16},{4,20},{8,24},{12,28},{16,0},{20,4},{24,8},{28,12},{1,17},{... | collective-permute-start | bytes 12296 | tf_op jit(solution)/shard_map/ppermute | solution.py:46
  111.1 1.6 %collective-permute-done.23 = f32[1,1024]{1,0:T(1,128)S(1)} collective-permute-done((f32[1,1024]{1,0:T(1,128)S(1)}, f32[1,1024]{1,0:T(1,128)S(1)}, u32[]{:S(2)}, u32[]{:S(2)}) %collective-permute-start.23) | collective-permute-done | bytes 4128 | tf_op jit(solution)/shard_map/ppermute | solution.py:46
  (59 shorter events, 21.9 us)
Async XLA Ops:
  0.0 21.9 %collective-permute-start.3 = (f32[1,2,96,1024]{3,2,1,0:T(8,128)}, f32[1,2,96,1024]{3,2,1,0:T(8,128)S(1)}, u32[]{:S(2)}, u32[]{:S(2)}) collective-permute-start(f32[1,2,96,1024]{3,2,1,0:T(8,128)} %own.9), channel_id=1, source_target_pairs={{0,8},{4,12},{8,24},{12,28},{24,16},{28,20},{16,0},{20,4},{1,9},{5... | collective-permute-start | bytes 2359304 | tf_op jit(solution)/shard_map/ppermute | solution.py:226
  3.1 39.5 %collective-permute-start.4 = (f32[1,2,96,1024]{3,2,1,0:T(8,128)}, f32[1,2,96,1024]{3,2,1,0:T(8,128)S(1)}, u32[]{:S(2)}, u32[]{:S(2)}) collective-permute-start(f32[1,2,96,1024]{3,2,1,0:T(8,128)} %own.9), channel_id=1, source_target_pairs={{0,16},{4,20},{8,0},{12,4},{24,8},{28,12},{16,24},{20,28},{1,17},{... | collective-permute-start | bytes 2359304 | tf_op jit(solution)/shard_map/ppermute | solution.py:227
  8.3 32.5 %collective-permute-start = (f32[192,768]{1,0:T(8,128)}, f32[192,768]{1,0:T(8,128)S(1)}, u32[]{:S(2)}, u32[]{:S(2)}) collective-permute-start(f32[192,768]{1,0:T(8,128)} %get-tuple-element.60.refs_0_), channel_id=1, source_target_pairs={{0,2},{2,0},{1,3},{3,1},{4,6},{6,4},{5,7},{7,5},{8,10},{10,8},{9,1... | collective-permute-start | bytes 1769480 | tf_op jit(solution)/shard_map/ppermute | solution.py:244
  10.1 30.7 %collective-permute-start.1 = (f32[192,768]{1,0:T(8,128)}, f32[192,768]{1,0:T(8,128)S(1)}, u32[]{:S(2)}, u32[]{:S(2)}) collective-permute-start(f32[192,768]{1,0:T(8,128)} %get-tuple-element.61), channel_id=1, source_target_pairs={{0,4},{4,0},{8,12},{12,8},{16,20},{20,16},{24,28},{28,24},{1,5},{5... | collective-permute-start | bytes 1769480 | tf_op jit(solution)/shard_map/ppermute | solution.py:245
  11.6 29.2 %collective-permute-start.2 = (f32[192,768]{1,0:T(8,128)}, f32[192,768]{1,0:T(8,128)S(1)}, u32[]{:S(2)}, u32[]{:S(2)}) collective-permute-start(f32[192,768]{1,0:T(8,128)} %get-tuple-element.61), channel_id=1, source_target_pairs={{0,6},{2,4},{4,2},{6,0},{8,14},{10,12},{12,10},{14,8},{16,22},{18,... | collective-permute-start | bytes 1769480 | tf_op jit(solution)/shard_map/ppermute | solution.py:246
  21.9 21.6 %collective-permute-start.5 = (f32[1,2,96,128]{3,2,1,0:T(8,128)S(1)}, f32[1,2,96,128]{3,2,1,0:T(8,128)S(1)}, u32[]{:S(2)}, u32[]{:S(2)}) collective-permute-start(f32[1,2,96,128]{3,2,1,0:T(8,128)S(1)} %get-tuple-element.116), channel_id=1, source_target_pairs={{0,8},{4,12},{8,24},{12,28},{24,16},{28,20},{16,0},{20,4},{1,9},{5... | collective-permute-start | bytes 294920 | tf_op jit(solution)/shard_map/ppermute | solution.py:256
  44.1 4.5 %collective-permute-start.6 = (f32[2,192,128]{2,1,0:T(8,128)S(1)}, f32[2,192,128]{2,1,0:T(8,128)S(1)}, u32[]{:S(2)}, u32[]{:S(2)}) collective-permute-start(f32[2,192,128]{2,1,0:T(8,128)S(1)} %get-tuple-element.68), channel_id=1, source_target_pairs={{0,1},{1,0},{2,3},{3,2},{4,5},{5,4},{6,7},{7,6},{8,9},{9,8},{10,11... | collective-permute-start | bytes 589832 | tf_op jit(solution)/shard_map/ppermute | solution.py:284
  44.2 8.7 %collective-permute-start.7 = (f32[1,2,96,256]{3,2,1,0:T(8,128)S(1)}, f32[1,2,96,256]{3,2,1,0:T(8,128)S(1)}, u32[]{:S(2)}, u32[]{:S(2)}) collective-permute-start(f32[1,2,96,256]{3,2,1,0:T(8,128)S(1)} %get-tuple-element.119), channel_id=1, source_target_pairs={{0,8},{4,12},{8,24},{12,28},{24,16},{28,20},{16,0},{20,4},{1,9},{5... | collective-permute-start | bytes 589832 | tf_op jit(solution)/shard_map/ppermute | solution.py:256
  53.4 3.4 %collective-permute-start.8 = (f32[2,192,256]{2,1,0:T(8,128)S(1)}, f32[2,192,256]{2,1,0:T(8,128)S(1)}, u32[]{:S(2)}, u32[]{:S(2)}) collective-permute-start(f32[2,192,256]{2,1,0:T(8,128)S(1)} %get-tuple-element.74), channel_id=1, source_target_pairs={{0,1},{1,0},{2,3},{3,2},{4,5},{5,4},{6,7},{7,6},{8,9},{9,8},{10,11... | collective-permute-start | bytes 1179656 | tf_op jit(solution)/shard_map/ppermute | solution.py:284
  53.4 8.5 %collective-permute-start.9 = (f32[1,2,96,256]{3,2,1,0:T(8,128)S(1)}, f32[1,2,96,256]{3,2,1,0:T(8,128)S(1)}, u32[]{:S(2)}, u32[]{:S(2)}) collective-permute-start(f32[1,2,96,256]{3,2,1,0:T(8,128)S(1)} %get-tuple-element.118), channel_id=1, source_target_pairs={{0,8},{4,12},{8,24},{12,28},{24,16},{28,20},{16,0},{20,4},{1,9},{5... | collective-permute-start | bytes 589832 | tf_op jit(solution)/shard_map/ppermute | solution.py:256
  62.4 3.1 %collective-permute-start.10 = (f32[2,192,256]{2,1,0:T(8,128)S(1)}, f32[2,192,256]{2,1,0:T(8,128)S(1)}, u32[]{:S(2)}, u32[]{:S(2)}) collective-permute-start(f32[2,192,256]{2,1,0:T(8,128)S(1)} %get-tuple-element.80), channel_id=1, source_target_pairs={{0,1},{1,0},{2,3},{3,2},{4,5},{5,4},{6,7},{7,6},{8,9},{9,8},{10,11... | collective-permute-start | bytes 1179656 | tf_op jit(solution)/shard_map/ppermute | solution.py:284
  62.5 8.2 %collective-permute-start.11 = (f32[1,2,96,256]{3,2,1,0:T(8,128)S(1)}, f32[1,2,96,256]{3,2,1,0:T(8,128)S(1)}, u32[]{:S(2)}, u32[]{:S(2)}) collective-permute-start(f32[1,2,96,256]{3,2,1,0:T(8,128)S(1)} %get-tuple-element.117), channel_id=1, source_target_pairs={{0,8},{4,12},{8,24},{12,28},{24,16},{28,20},{16,0},{20,4},{1,9},{5... | collective-permute-start | bytes 589832 | tf_op jit(solution)/shard_map/ppermute | solution.py:256
  71.1 3.0 %collective-permute-start.12 = (f32[2,192,256]{2,1,0:T(8,128)S(1)}, f32[2,192,256]{2,1,0:T(8,128)S(1)}, u32[]{:S(2)}, u32[]{:S(2)}) collective-permute-start(f32[2,192,256]{2,1,0:T(8,128)S(1)} %get-tuple-element.86), channel_id=1, source_target_pairs={{0,1},{1,0},{2,3},{3,2},{4,5},{5,4},{6,7},{7,6},{8,9},{9,8},{10,11... | collective-permute-start | bytes 1179656 | tf_op jit(solution)/shard_map/ppermute | solution.py:284
  71.2 6.1 %collective-permute-start.13 = (f32[1,2,96,128]{3,2,1,0:T(8,128)S(1)}, f32[1,2,96,128]{3,2,1,0:T(8,128)S(1)}, u32[]{:S(2)}, u32[]{:S(2)}) collective-permute-start(f32[1,2,96,128]{3,2,1,0:T(8,128)S(1)} %get-tuple-element.115), channel_id=1, source_target_pairs={{0,8},{4,12},{8,24},{12,28},{24,16},{28,20},{16,0},{20,4},{1,9},{5... | collective-permute-start | bytes 294920 | tf_op jit(solution)/shard_map/ppermute | solution.py:256
  77.8 4.2 %collective-permute-start.14 = (f32[2,192,128]{2,1,0:T(8,128)S(1)}, f32[2,192,128]{2,1,0:T(8,128)S(1)}, u32[]{:S(2)}, u32[]{:S(2)}) collective-permute-start(f32[2,192,128]{2,1,0:T(8,128)S(1)} %get-tuple-element.93), channel_id=1, source_target_pairs={{0,1},{1,0},{2,3},{3,2},{4,5},{5,4},{6,7},{7,6},{8,9},{9,8},{10,11... | collective-permute-start | bytes 589832 | tf_op jit(solution)/shard_map/ppermute | solution.py:284
  77.9 7.8 %collective-permute-start.16 = (f32[192,256]{1,0:T(8,128)S(1)}, f32[192,256]{1,0:T(8,128)S(1)}, u32[]{:S(2)}, u32[]{:S(2)}) collective-permute-start(f32[192,256]{1,0:T(8,128)S(1)} %get-tuple-element.90), channel_id=1, source_target_pairs={{0,4},{4,0},{8,12},{12,8},{16,20},{20,16},{24,28},{28,24},{1,5},{5... | collective-permute-start | bytes 589832 | tf_op jit(solution)/shard_map/ppermute | solution.py:290
  79.5 10.5 %collective-permute-start.17 = (f32[192,256]{1,0:T(8,128)S(1)}, f32[192,256]{1,0:T(8,128)S(1)}, u32[]{:S(2)}, u32[]{:S(2)}) collective-permute-start(f32[192,256]{1,0:T(8,128)S(1)} %get-tuple-element.84), channel_id=1, source_target_pairs={{0,4},{4,0},{8,12},{12,8},{16,20},{20,16},{24,28},{28,24},{1,5},{5... | collective-permute-start | bytes 589832 | tf_op jit(solution)/shard_map/ppermute | solution.py:290
  80.0 14.2 %collective-permute-start.18 = (f32[192,256]{1,0:T(8,128)S(1)}, f32[192,256]{1,0:T(8,128)S(1)}, u32[]{:S(2)}, u32[]{:S(2)}) collective-permute-start(f32[192,256]{1,0:T(8,128)S(1)} %get-tuple-element.78), channel_id=1, source_target_pairs={{0,4},{4,0},{8,12},{12,8},{16,20},{20,16},{24,28},{28,24},{1,5},{5... | collective-permute-start | bytes 589832 | tf_op jit(solution)/shard_map/ppermute | solution.py:290
  81.5 14.8 %collective-permute-start.19 = (f32[192,128]{1,0:T(8,128)S(1)}, f32[192,128]{1,0:T(8,128)S(1)}, u32[]{:S(2)}, u32[]{:S(2)}) collective-permute-start(f32[192,128]{1,0:T(8,128)S(1)} %get-tuple-element.72), channel_id=1, source_target_pairs={{0,4},{4,0},{8,12},{12,8},{16,20},{20,16},{24,28},{28,24},{1,5},{5... | collective-permute-start | bytes 294920 | tf_op jit(solution)/shard_map/ppermute | solution.py:290
  82.0 16.7 %collective-permute-start.15 = (f32[192,128]{1,0:T(8,128)S(1)}, f32[192,128]{1,0:T(8,128)S(1)}, u32[]{:S(2)}, u32[]{:S(2)}) collective-permute-start(f32[192,128]{1,0:T(8,128)S(1)} %get-tuple-element.95), channel_id=1, source_target_pairs={{0,4},{4,0},{8,12},{12,8},{16,20},{20,16},{24,28},{28,24},{1,5},{5... | collective-permute-start | bytes 294920 | tf_op jit(solution)/shard_map/ppermute | solution.py:290
  99.4 1.2 %collective-permute-start.20 = (f32[1,1024]{1,0:T(1,128)S(1)}, f32[1,1024]{1,0:T(1,128)S(1)}, u32[]{:S(2)}, u32[]{:S(2)}) collective-permute-start(f32[1,1024]{1,0:T(1,128)S(1)} %get-tuple-element.109), channel_id=1, source_target_pairs={{0,1},{1,0},{2,3},{3,2},{4,5},{5,4},{6,7},{7,6},{8,9},{9,8},{10,11... | collective-permute-start | bytes 12296 | tf_op jit(solution)/shard_map/ppermute | solution.py:46
  100.6 3.6 %collective-permute-start.21 = (f32[1,1024]{1,0:T(1,128)S(1)}, f32[1,1024]{1,0:T(1,128)S(1)}, u32[]{:S(2)}, u32[]{:S(2)}) collective-permute-start(f32[1,1024]{1,0:T(1,128)S(1)} %add.12), channel_id=1, source_target_pairs={{0,4},{4,0},{8,12},{12,8},{16,20},{20,16},{24,28},{28,24},{1,5},{5... | collective-permute-start | bytes 12296 | tf_op jit(solution)/shard_map/ppermute | solution.py:46
  104.2 3.6 %collective-permute-start.22 = (f32[1,1024]{1,0:T(1,128)S(1)}, f32[1,1024]{1,0:T(1,128)S(1)}, u32[]{:S(2)}, u32[]{:S(2)}) collective-permute-start(f32[1,1024]{1,0:T(1,128)S(1)} %add.13), channel_id=1, source_target_pairs={{0,8},{4,12},{8,0},{12,4},{16,24},{20,28},{24,16},{28,20},{1,9},{5... | collective-permute-start | bytes 12296 | tf_op jit(solution)/shard_map/ppermute | solution.py:46
  107.9 4.8 %collective-permute-start.23 = (f32[1,1024]{1,0:T(1,128)S(1)}, f32[1,1024]{1,0:T(1,128)S(1)}, u32[]{:S(2)}, u32[]{:S(2)}) collective-permute-start(f32[1,1024]{1,0:T(1,128)S(1)} %add.14), channel_id=1, source_target_pairs={{0,16},{4,20},{8,24},{12,28},{16,0},{20,4},{24,8},{28,12},{1,17},{... | collective-permute-start | bytes 12296 | tf_op jit(solution)/shard_map/ppermute | solution.py:46
  (3 other events, 43.8 us)

commit v2 on v1

--- a/solution.py
+++ b/solution.py
@@ -92,39 +92,47 @@
     return dot(a_high, b_high) + (dot(a_high, b_low) + dot(a_low, b_high))
 
 
-def left_kernel(steps, rows, pattern, source, mine, other, turned):
-    group, _, sections, width = source.shape
+def left_kernel(steps, pattern, source, mine, other, turned):
+    rows, _, sections, width = source.shape
     n_row, row = lax.axis_size("row"), lax.axis_index("row")
     depth = width // n_row
-    block_row = (lax.axis_index("col") * rows + pl.program_id(0) * group) // BLK
-    for s in range(sections):
-        kept = []
-        for w in range(width // BLK):
-            keep = pattern[block_row, 0, s, w]
-            kept.append(jnp.where(keep != 0, source[:, 0, s, pl.ds(w * BLK, BLK)], 0.0))
-        value = jnp.concatenate(kept, axis=1)
-        for r in range(n_row):
-            turned[r, s] = value[:, r * depth : (r + 1) * depth]
-    for out, parity in ((mine, row % 2), (other, 1 - row % 2)):
-        owners = [line_at(row // 2, step) * 2 + parity for step in steps]
-        pieces = [turned[r, s] for r in owners for s in range(sections)]
-        out[...] = jnp.concatenate(pieces, axis=1)
-
-
-def order_kernel(cuts, *refs):
-    pieces, outs = refs[:4], refs[4:]
-    rows = pieces[0].shape[0]
+    group = 64
+    for g in range(rows // group):
+        part = pl.ds(g * group, group)
+        block_row = (lax.axis_index("col") * rows + g * group) // BLK
+        for s in range(sections):
+            kept = []
+            for w in range(width // BLK):
+                keep = pattern[block_row, 0, s, w]
+                piece = source[part, 0, s, pl.ds(w * BLK, BLK)]
+                kept.append(jnp.where(keep != 0, piece, 0.0))
+            value = jnp.concatenate(kept, axis=1)
+            for r in range(n_row):
+                turned[r, s, part, :] = value[:, r * depth : (r + 1) * depth]
+        for out, parity in ((mine, row % 2), (other, 1 - row % 2)):
+            owners = [line_at(row // 2, step) * 2 + parity for step in steps]
+            pieces = [turned[r, s, part, :] for r in owners for s in range(sections)]
+            out[part, :] = jnp.concatenate(pieces, axis=1)
+
+
+def order_kernel(cuts, own_x, other_x, *outs):
+    rows = own_x.shape[0]
     flip = lax.axis_index("col") ^ lax.axis_index("fiber")
-    for p, piece in enumerate(pieces):
-        y, x = divmod(p, 2)
-        start = pl.multiple_of((y + 2 * (x ^ flip)) * rows, rows)
-        for i, (low_end, high_end) in enumerate(cuts):
-            high, low = split(piece[:, low_end:high_end])
+    for x, piece in enumerate((own_x, other_x)):
+        start = pl.multiple_of((x ^ flip) * rows, rows)
+        for i, (first, last) in enumerate(cuts):
+            high, low = split(piece[:, first:last])
             outs[2 * i][pl.ds(start, rows), :] = high
             outs[2 * i + 1][pl.ds(start, rows), :] = low
 
 
-def near_kernel(first, own_high, own_low, high, low, own, down, up, out, b_high, b_low):
+def stacked(early, late):
+    return jnp.concatenate([early[...], late[...]], axis=0)
+
+
+def near_kernel(first, *refs):
+    lefts, (down, up, own, out, b_high, b_low) = refs[:8], refs[8:]
+    high, low, own_high, own_low = (stacked(*lefts[2 * i : 2 * i + 2]) for i in range(4))
     _, sections, depth, _ = own.shape
     tile = slice(first, first + out.shape[1])
     for i, shard in enumerate((down, up, own)):
@@ -132,21 +140,23 @@
             part = pl.ds((i * sections + s) * depth, depth)
             b_high[part, :], b_low[part, :] = split(shard[0, s, :, tile])
     cut = 2 * sections * depth
-    total = product3(high[...], low[...], b_high[:cut, :], b_low[:cut, :])
-    out[...] = total + product3(own_high[...], own_low[...], b_high[cut:, :], b_low[cut:, :])
-
-
-def far_kernel(high, low, near, shard, kept, sent, b_high, b_low):
+    total = product3(high, low, b_high[:cut, :], b_low[:cut, :])
+    out[...] = total + product3(own_high, own_low, b_high[cut:, :], b_low[cut:, :])
+
+
+def far_kernel(*refs):
+    lefts, (near, shard, kept, sent, b_high, b_low) = refs[:4], refs[4:]
+    high, low = stacked(*lefts[:2]), stacked(*lefts[2:])
     _, sections, depth, _ = shard.shape
     rows = kept.shape[1]
     for s in range(sections):
         part = pl.ds(s * depth, depth)
         b_high[part, :], b_low[part, :] = split(shard[0, s])
-    value = product3(high[...], low[...], b_high[...], b_low[...])
-    for q in range(4):
-        out = sent if q >= 2 else kept
-        block = pl.ds(q * rows, rows)
-        out[q % 2] = near[block, :] + value[q * rows : (q + 1) * rows]
+    value = product3(high, low, b_high[...], b_low[...])
+    for block in range(4):
+        y, x = divmod(block, 2)
+        out = sent if x else kept
+        out[y] = near[pl.ds(block * rows, rows), :] + value[block * rows : (block + 1) * rows]
 
 
 def fold_kernel(kept, received, mine, other):
@@ -154,34 +164,30 @@
     other[...] = kept[1] + received[1]
 
 
-def square_kernel(first, pattern, mine, received, *refs):
-    *before, squares, sums = refs
-    share, columns = mine.shape
+def square_kernel(count, pattern, *refs):
+    mine, received, (squares, sums) = refs[:count], refs[count : 2 * count], refs[2 * count :]
+    share = squares.shape[0]
     fiber = lax.axis_index("fiber")
     group = 64
-    for w in range(columns // BLK):
-        tile = pl.ds(w * BLK, BLK)
-        total = jnp.zeros((8, BLK), jnp.float32)
-        for g in range(share // group):
-            keep = pattern[(fiber * share + g * group) // BLK, first // BLK + w]
-            part = pl.ds(g * group, group)
-            value = mine[part, tile] + received[part, tile]
-            value = jnp.where(keep != 0, value, 0.0)
-            value = value * value
-            squares[part, tile] = value
-            total += jnp.sum(value.reshape(group // 8, 8, BLK), axis=0)
-        sums[:, pl.ds(first + w * BLK, BLK)] = jnp.sum(total, axis=0, keepdims=True)
-    for old in before:
-        sums[:, :first] = old[...]
-
-
-def scale_kernel(row_total, sums, *refs):
-    *chunks, out = refs
     first = 0
-    for chunk in chunks:
-        tile = pl.ds(first, chunk.shape[1])
-        out[:, tile] = chunk[...] / (sums[:, tile] / row_total + EPS)
-        first += chunk.shape[1]
+    for ours, theirs in zip(mine, received, strict=True):
+        for w in range(ours.shape[1] // BLK):
+            tile, place = pl.ds(w * BLK, BLK), pl.ds(first + w * BLK, BLK)
+            total = jnp.zeros((8, BLK), jnp.float32)
+            for g in range(share // group):
+                keep = pattern[(fiber * share + g * group) // BLK, first // BLK + w]
+                part = pl.ds(g * group, group)
+                value = ours[part, tile] + theirs[part, tile]
+                value = jnp.where(keep != 0, value, 0.0)
+                value = value * value
+                squares[part, place] = value
+                total += jnp.sum(value.reshape(group // 8, 8, BLK), axis=0)
+            sums[:, place] = jnp.sum(total, axis=0, keepdims=True)
+        first += ours.shape[1]
+
+
+def scale_kernel(row_total, sums, squares, out):
+    out[...] = squares[...] / (sums[...] / row_total + EPS)
 
 
 def together(*values):
@@ -227,16 +233,11 @@
     up = lax.ppermute(b_panels, "row", line_pairs(-1))
 
     steps = (-1, 1, 0, 2)
-    group = 64
-    blocked = pl.BlockSpec((group, half), lambda i: (i, 0))
     mine, other = call(
-        functools.partial(left_kernel, steps, rows),
+        functools.partial(left_kernel, steps),
         [shape((rows, half), f32)] * 2,
-        [SMEM, pl.BlockSpec((group, 1, sections, width), lambda i: (i, 0, 0, 0))],
-        [pltpu.VMEM((n_row, sections, group, depth), f32)],
-        limit=56,
-        grid=(rows // group,),
-        out_specs=[blocked] * 2,
+        [SMEM, VMEM],
+        [pltpu.VMEM((n_row, sections, rows, depth), f32)],
     )(a_pattern, a_panels)
     swap = [(0, 1), (1, 0)]
     swap_y = [(r, r ^ 1) for r in range(n_row)]
@@ -245,11 +246,17 @@
     from_y = lax.ppermute(other, "row", swap_y)
     from_both = lax.ppermute(other, ("row", "col"), swap_both)
     cuts = ((0, 2 * shard_depth), (2 * shard_depth, 3 * shard_depth), (3 * shard_depth, half))
-    near_high, near_low, own_high, own_low, far_high, far_low = call(
-        functools.partial(order_kernel, cuts),
-        [shape((plane_rows, b - a), bf16) for a, b in cuts for _ in range(2)],
-        [VMEM] * 4,
-    )(mine, from_x, from_y, from_both)
+
+    def ordered(*pieces):
+        return call(
+            functools.partial(order_kernel, cuts),
+            [shape((2 * rows, b - a), bf16) for a, b in cuts for _ in range(2)],
+            [VMEM] * 2,
+        )(*pieces)
+
+    lefts = list(zip(ordered(mine, from_x), ordered(from_y, from_both), strict=True))
+    near_lefts = [part for pair in lefts[:4] for part in pair]
+    far_lefts = [part for pair in lefts[4:] for part in pair]
 
     starts = [sum(CHUNKS[:j]) for j in range(len(CHUNKS))]
     far = [
@@ -262,10 +269,10 @@
         (total,) = call(
             functools.partial(near_kernel, starts[j]),
             [shape((plane_rows, CHUNKS[j]), f32)],
-            [VMEM] * 7,
+            [VMEM] * 11,
             [factor, factor],
             6 * plane_rows * CHUNKS[j] * 3 * shard_depth,
-        )(own_high, own_low, near_high, near_low, b_panels, down, up)
+        )(*near_lefts, down, up, b_panels)
         return total
 
     ends = []
@@ -277,10 +284,10 @@
         kept, sent = call(
             far_kernel,
             [shape((2, rows, chunk), f32)] * 2,
-            [VMEM] * 4,
+            [VMEM] * 6,
             [factor, factor],
             6 * plane_rows * chunk * shard_depth,
-        )(far_high, far_low, near, shard)
+        )(*far_lefts, near, shard)
         received = lax.ppermute(sent, "fiber", swap)
         if j + 1 < len(CHUNKS):
             near = near_product(j + 1)
@@ -288,22 +295,17 @@
         stays, goes = call(fold_kernel, [shape((rows, chunk), f32)] * 2, [VMEM] * 2)(kept, received)
         ends.append(goes)
         far[j] = stays, lax.ppermute(goes, "row", swap_y)
-    squares, sums = [], []
-    for j, (stays, received) in enumerate(far):
-        received, _ = together(received, ends[-1])
-        square, total = call(
-            functools.partial(square_kernel, starts[j]),
-            [shape((rows, CHUNKS[j]), f32), shape((1, starts[j] + CHUNKS[j]), f32)],
-            [SMEM] + [VMEM] * (2 + len(sums)),
-        )(c_pattern, stays, received, *sums)
-        squares.append(square)
-        sums = [total]
-    total = all_sum(all_sum(sums[0], "fiber"), "row")
+    squares, sums = call(
+        functools.partial(square_kernel, len(far)),
+        [shape((share, columns), f32), shape((1, columns), f32)],
+        [SMEM] + [VMEM] * (2 * len(far)),
+    )(c_pattern, *(stays for stays, _ in far), *(received for _, received in far))
+    total = all_sum(all_sum(sums, "fiber"), "row")
     (out,) = call(
         functools.partial(scale_kernel, share * fibers * n_row),
         [shape((share, columns), f32)],
-        [VMEM] * (1 + len(squares)),
-    )(total, *squares)
+        [VMEM] * 2,
+    )(total, squares)
     return out
 
 
@@ -315,4 +317,6 @@
         P("row", "col"),
     )
 
-    return jax.shard_map(local, mesh=mesh, in_specs=placed, out_specs=P(("row", "fiber"), "col"), check_vma=False)
+    return jax.shard_map(
+        local, mesh=mesh, in_specs=placed, out_specs=P(("row", "fiber"), "col"), check_vma=False
+    )

time: 114 us -> 113 us (level)
  Pallas kernels: 16.6 us -> 12.5 us
  waiting for transfers between devices: 46.9 us -> 49.2 us
    pallas_call x23 -> x20, Pallas kernels: 16.6 us -> 12.5 us  [run(): pl.pallas_call(kernel, out_shape=out_shapes, in_specs=specs, scratch_shap...]
    ppermute x5, waiting for transfers between devices: 12.6 us -> 14.2 us  [local(): far[j] = (stays, lax.ppermute(goes, 'row', swap_y))]
  transfers between devices with their start and end apart: 24 -> 24, of which waited for: 13 -> 12; matrix products, arithmetic and copies ran while one was open for 0% -> 0% of each run, Pallas kernels for 11% -> 8%
where the time goes in v2:
time: 113 us
  waiting for transfers between devices  49.2 us (44%)
  starting transfers between devices  48.7 us (43%)
  Pallas kernels  12.5 us (11%)
  local copies, waits for them, and re-layouts  2.02 us (2%)
    ppermute x5, starting transfers between devices, local(): lax.ppermute(down[..., first:first + chunk], 'row', line_pairs(1))  28.3 us
    ppermute x5, waiting for transfers between devices, local(): lax.ppermute(down[..., first:first + chunk], 'row', line_pairs(1))  18.6 us
    ppermute x5, waiting for transfers between devices, local(): far[j] = (stays, lax.ppermute(goes, 'row', swap_y))  14.2 us
    pallas_call x20, Pallas kernels, run(): pl.pallas_call(kernel, out_shape=out_shapes, in_specs=specs, scratch_shap...  12.5 us
    ppermute x1, waiting for transfers between devices, local(): down = lax.ppermute(b_panels, 'row', line_pairs(1))  9.91 us
    ppermute x4, starting transfers between devices, all_sum(): total = total + lax.ppermute(value, axis_name, pairs)  6.75 us
    ppermute x4, waiting for transfers between devices, all_sum(): total = total + lax.ppermute(value, axis_name, pairs)  6.53 us
    ppermute x5, starting transfers between devices, local(): far[j] = (stays, lax.ppermute(goes, 'row', swap_y))  5.7 us
  transfers between devices with their start and end apart: 24, of which 12 were waited for; matrix products, arithmetic and copies ran while one was open for 0% of the time, Pallas kernels for 8%

profile of v2, /device:TPU:0, one launch (start us, length us, event | category | flops | bytes accessed | tf_op | source)
XLA Modules:
  0.0 112.8 jit_solution(17095783166804887943)
XLA Ops:
  0.0 3.1 %collective-permute-start.3 = (f32[1,2,96,1024]{3,2,1,0:T(8,128)}, f32[1,2,96,1024]{3,2,1,0:T(8,128)S(1)}, u32[]{:S(2)}, u32[]{:S(2)}) collective-permute-start(f32[1,2,96,1024]{3,2,1,0:T(8,128)} %refs_10_.9), channel_id=1, source_target_pairs={{0,8},{4,12},{8,24},{12,28},{24,16},{28,20},{16,0},{20,4},{1,9},{5... | collective-permute-start | bytes 2359304 | tf_op jit(solution)/shard_map/ppermute | solution.py:232
  6.0 2.4 %shard_map.46 = (f32[192,768]{1,0:T(8,128)S(1)}, f32[192,768]{1,0:T(8,128)S(1)}) custom-call(s32[3,1,2,6]{3,2,1,0:T(2,128)S(1)} %copy-done.2, f32[192,1,2,768]{3,2,1,0:T(2,128)S(1)} %copy-done.1), custom_call_target="tpu_custom_call" | custom-call | bytes 2359440 | tf_op jit(solution)/shard_map/pallas_call | solution.py:204
  8.4 1.9 %collective-permute-start = (f32[192,768]{1,0:T(8,128)S(1)}, f32[192,768]{1,0:T(8,128)S(1)}, u32[]{:S(2)}, u32[]{:S(2)}) collective-permute-start(f32[192,768]{1,0:T(8,128)S(1)} %get-tuple-element.53.own_x), channel_id=1, source_target_pairs={{0,2},{2,0},{1,3},{3,1},{4,6},{6,4},{5,7},{7,5},{8,10},{10,8},{9,1... | collective-permute-start | bytes 1769480 | tf_op jit(solution)/shard_map/ppermute | solution.py:245
  10.3 1.5 %collective-permute-start.1 = (f32[192,768]{1,0:T(8,128)S(1)}, f32[192,768]{1,0:T(8,128)S(1)}, u32[]{:S(2)}, u32[]{:S(2)}) collective-permute-start(f32[192,768]{1,0:T(8,128)S(1)} %get-tuple-element.55), channel_id=1, source_target_pairs={{0,4},{4,0},{8,12},{12,8},{16,20},{20,16},{24,28},{28,24},{1,5},{5... | collective-permute-start | bytes 1769480 | tf_op jit(solution)/shard_map/ppermute | solution.py:246
  12.0 9.9 %collective-permute-done.3.refs_8_ = f32[1,2,96,1024]{3,2,1,0:T(8,128)S(1)} collective-permute-done((f32[1,2,96,1024]{3,2,1,0:T(8,128)}, f32[1,2,96,1024]{3,2,1,0:T(8,128)S(1)}, u32[]{:S(2)}, u32[]{:S(2)}) %collective-permute-start.3) | collective-permute-done | bytes 786464 | tf_op jit(solution)/shard_map/ppermute | solution.py:232
  21.9 18.8 %collective-permute-start.5 = (f32[1,2,96,128]{3,2,1,0:T(8,128)S(1)}, f32[1,2,96,128]{3,2,1,0:T(8,128)S(1)}, u32[]{:S(2)}, u32[]{:S(2)}) collective-permute-start(f32[1,2,96,128]{3,2,1,0:T(8,128)S(1)} %get-tuple-element.102), channel_id=1, source_target_pairs={{0,8},{4,12},{8,24},{12,28},{24,16},{28,20},{16,0},{20,4},{1,9},{5... | collective-permute-start | bytes 294920 | tf_op jit(solution)/shard_map/ppermute | solution.py:263
  43.6 3.3 %collective-permute-start.7 = (f32[1,2,96,256]{3,2,1,0:T(8,128)S(1)}, f32[1,2,96,256]{3,2,1,0:T(8,128)S(1)}, u32[]{:S(2)}, u32[]{:S(2)}) collective-permute-start(f32[1,2,96,256]{3,2,1,0:T(8,128)S(1)} %get-tuple-element.105), channel_id=1, source_target_pairs={{0,8},{4,12},{8,24},{12,28},{24,16},{28,20},{16,0},{20,4},{1,9},{5... | collective-permute-start | bytes 589832 | tf_op jit(solution)/shard_map/ppermute | solution.py:263
  48.1 4.8 %collective-permute-done.7.refs_5_ = f32[1,2,96,256]{3,2,1,0:T(8,128)S(1)} collective-permute-done((f32[1,2,96,256]{3,2,1,0:T(8,128)S(1)}, f32[1,2,96,256]{3,2,1,0:T(8,128)S(1)}, u32[]{:S(2)}, u32[]{:S(2)}) %collective-permute-start.7) | collective-permute-done | bytes 196640 | tf_op jit(solution)/shard_map/ppermute | solution.py:263
  53.4 2.2 %collective-permute-start.9 = (f32[1,2,96,256]{3,2,1,0:T(8,128)S(1)}, f32[1,2,96,256]{3,2,1,0:T(8,128)S(1)}, u32[]{:S(2)}, u32[]{:S(2)}) collective-permute-start(f32[1,2,96,256]{3,2,1,0:T(8,128)S(1)} %get-tuple-element.104), channel_id=1, source_target_pairs={{0,8},{4,12},{8,24},{12,28},{24,16},{28,20},{16,0},{20,4},{1,9},{5... | collective-permute-start | bytes 589832 | tf_op jit(solution)/shard_map/ppermute | solution.py:263
  56.8 5.1 %collective-permute-done.9.refs_5_ = f32[1,2,96,256]{3,2,1,0:T(8,128)S(1)} collective-permute-done((f32[1,2,96,256]{3,2,1,0:T(8,128)S(1)}, f32[1,2,96,256]{3,2,1,0:T(8,128)S(1)}, u32[]{:S(2)}, u32[]{:S(2)}) %collective-permute-start.9) | collective-permute-done | bytes 196640 | tf_op jit(solution)/shard_map/ppermute | solution.py:263
  62.5 2.0 %collective-permute-start.11 = (f32[1,2,96,256]{3,2,1,0:T(8,128)S(1)}, f32[1,2,96,256]{3,2,1,0:T(8,128)S(1)}, u32[]{:S(2)}, u32[]{:S(2)}) collective-permute-start(f32[1,2,96,256]{3,2,1,0:T(8,128)S(1)} %get-tuple-element.103), channel_id=1, source_target_pairs={{0,8},{4,12},{8,24},{12,28},{24,16},{28,20},{16,0},{20,4},{1,9},{5... | collective-permute-start | bytes 589832 | tf_op jit(solution)/shard_map/ppermute | solution.py:263
  65.6 5.1 %collective-permute-done.11.refs_5_ = f32[1,2,96,256]{3,2,1,0:T(8,128)S(1)} collective-permute-done((f32[1,2,96,256]{3,2,1,0:T(8,128)S(1)}, f32[1,2,96,256]{3,2,1,0:T(8,128)S(1)}, u32[]{:S(2)}, u32[]{:S(2)}) %collective-permute-start.11) | collective-permute-done | bytes 196640 | tf_op jit(solution)/shard_map/ppermute | solution.py:263
  71.2 2.0 %collective-permute-start.13 = (f32[1,2,96,128]{3,2,1,0:T(8,128)S(1)}, f32[1,2,96,128]{3,2,1,0:T(8,128)S(1)}, u32[]{:S(2)}, u32[]{:S(2)}) collective-permute-start(f32[1,2,96,128]{3,2,1,0:T(8,128)S(1)} %get-tuple-element.101), channel_id=1, source_target_pairs={{0,8},{4,12},{8,24},{12,28},{24,16},{28,20},{16,0},{20,4},{1,9},{5... | collective-permute-start | bytes 294920 | tf_op jit(solution)/shard_map/ppermute | solution.py:263
  74.2 3.1 %collective-permute-done.13.refs_5_ = f32[1,2,96,128]{3,2,1,0:T(8,128)S(1)} collective-permute-done((f32[1,2,96,128]{3,2,1,0:T(8,128)S(1)}, f32[1,2,96,128]{3,2,1,0:T(8,128)S(1)}, u32[]{:S(2)}, u32[]{:S(2)}) %collective-permute-start.13) | collective-permute-done | bytes 98336 | tf_op jit(solution)/shard_map/ppermute | solution.py:263
  77.9 1.6 %collective-permute-start.16 = (f32[192,256]{1,0:T(8,128)S(1)}, f32[192,256]{1,0:T(8,128)S(1)}, u32[]{:S(2)}, u32[]{:S(2)}) collective-permute-start(f32[192,256]{1,0:T(8,128)S(1)} %get-tuple-element.79), channel_id=1, source_target_pairs={{0,4},{4,0},{8,12},{12,8},{16,20},{20,16},{24,28},{28,24},{1,5},{5... | collective-permute-start | bytes 589832 | tf_op jit(solution)/shard_map/ppermute | solution.py:297
  80.0 1.5 %collective-permute-start.18 = (f32[192,256]{1,0:T(8,128)S(1)}, f32[192,256]{1,0:T(8,128)S(1)}, u32[]{:S(2)}, u32[]{:S(2)}) collective-permute-start(f32[192,256]{1,0:T(8,128)S(1)} %get-tuple-element.93), channel_id=1, source_target_pairs={{0,4},{4,0},{8,12},{12,8},{16,20},{20,16},{24,28},{28,24},{1,5},{5... | collective-permute-start | bytes 589832 | tf_op jit(solution)/shard_map/ppermute | solution.py:297
  82.0 1.6 %collective-permute-start.19 = (f32[192,128]{1,0:T(8,128)S(1)}, f32[192,128]{1,0:T(8,128)S(1)}, u32[]{:S(2)}, u32[]{:S(2)}) collective-permute-start(f32[192,128]{1,0:T(8,128)S(1)} %get-tuple-element.98), channel_id=1, source_target_pairs={{0,4},{4,0},{8,12},{12,8},{16,20},{20,16},{24,28},{28,24},{1,5},{5... | collective-permute-start | bytes 294920 | tf_op jit(solution)/shard_map/ppermute | solution.py:297
  83.6 12.6 %collective-permute-done.15.refs_5_ = f32[192,128]{1,0:T(8,128)S(1)} collective-permute-done((f32[192,128]{1,0:T(8,128)S(1)}, f32[192,128]{1,0:T(8,128)S(1)}, u32[]{:S(2)}, u32[]{:S(2)}) %collective-permute-start.15) | collective-permute-done | bytes 98336 | tf_op jit(solution)/shard_map/ppermute | solution.py:297
  96.3 1.6 %collective-permute-done.19.refs_9_ = f32[192,128]{1,0:T(8,128)S(1)} collective-permute-done((f32[192,128]{1,0:T(8,128)S(1)}, f32[192,128]{1,0:T(8,128)S(1)}, u32[]{:S(2)}, u32[]{:S(2)}) %collective-permute-start.19) | collective-permute-done | bytes 98336 | tf_op jit(solution)/shard_map/ppermute | solution.py:297
  101.3 2.1 %collective-permute-done.21 = f32[1,1024]{1,0:T(1,128)S(1)} collective-permute-done((f32[1,1024]{1,0:T(1,128)S(1)}, f32[1,1024]{1,0:T(1,128)S(1)}, u32[]{:S(2)}, u32[]{:S(2)}) %collective-permute-start.21) | collective-permute-done | bytes 4128 | tf_op jit(solution)/shard_map/ppermute | solution.py:46
  103.4 1.9 %collective-permute-start.22 = (f32[1,1024]{1,0:T(1,128)S(1)}, f32[1,1024]{1,0:T(1,128)S(1)}, u32[]{:S(2)}, u32[]{:S(2)}) collective-permute-start(f32[1,1024]{1,0:T(1,128)S(1)} %add.13), channel_id=1, source_target_pairs={{0,8},{4,12},{8,0},{12,4},{16,24},{20,28},{24,16},{28,20},{1,9},{5... | collective-permute-start | bytes 12296 | tf_op jit(solution)/shard_map/ppermute | solution.py:46
  105.3 1.7 %collective-permute-done.22 = f32[1,1024]{1,0:T(1,128)S(1)} collective-permute-done((f32[1,1024]{1,0:T(1,128)S(1)}, f32[1,1024]{1,0:T(1,128)S(1)}, u32[]{:S(2)}, u32[]{:S(2)}) %collective-permute-start.22) | collective-permute-done | bytes 4128 | tf_op jit(solution)/shard_map/ppermute | solution.py:46
  107.0 3.3 %collective-permute-start.23 = (f32[1,1024]{1,0:T(1,128)S(1)}, f32[1,1024]{1,0:T(1,128)S(1)}, u32[]{:S(2)}, u32[]{:S(2)}) collective-permute-start(f32[1,1024]{1,0:T(1,128)S(1)} %add.14), channel_id=1, source_target_pairs={{0,16},{4,20},{8,24},{12,28},{16,0},{20,4},{24,8},{28,12},{1,17},{... | collective-permute-start | bytes 12296 | tf_op jit(solution)/shard_map/ppermute | solution.py:46
  110.3 1.6 %collective-permute-done.23 = f32[1,1024]{1,0:T(1,128)S(1)} collective-permute-done((f32[1,1024]{1,0:T(1,128)S(1)}, f32[1,1024]{1,0:T(1,128)S(1)}, u32[]{:S(2)}, u32[]{:S(2)}) %collective-permute-start.23) | collective-permute-done | bytes 4128 | tf_op jit(solution)/shard_map/ppermute | solution.py:46
  (58 shorter events, 17.8 us)
Async XLA Ops:
  0.0 21.9 %collective-permute-start.3 = (f32[1,2,96,1024]{3,2,1,0:T(8,128)}, f32[1,2,96,1024]{3,2,1,0:T(8,128)S(1)}, u32[]{:S(2)}, u32[]{:S(2)}) collective-permute-start(f32[1,2,96,1024]{3,2,1,0:T(8,128)} %refs_10_.9), channel_id=1, source_target_pairs={{0,8},{4,12},{8,24},{12,28},{24,16},{28,20},{16,0},{20,4},{1,9},{5... | collective-permute-start | bytes 2359304 | tf_op jit(solution)/shard_map/ppermute | solution.py:232
  3.1 38.5 %collective-permute-start.4 = (f32[1,2,96,1024]{3,2,1,0:T(8,128)}, f32[1,2,96,1024]{3,2,1,0:T(8,128)S(1)}, u32[]{:S(2)}, u32[]{:S(2)}) collective-permute-start(f32[1,2,96,1024]{3,2,1,0:T(8,128)} %refs_10_.9), channel_id=1, source_target_pairs={{0,16},{4,20},{8,0},{12,4},{24,8},{28,12},{16,24},{20,28},{1,17},{... | collective-permute-start | bytes 2359304 | tf_op jit(solution)/shard_map/ppermute | solution.py:233
  8.4 32.3 %collective-permute-start = (f32[192,768]{1,0:T(8,128)S(1)}, f32[192,768]{1,0:T(8,128)S(1)}, u32[]{:S(2)}, u32[]{:S(2)}) collective-permute-start(f32[192,768]{1,0:T(8,128)S(1)} %get-tuple-element.53.own_x), channel_id=1, source_target_pairs={{0,2},{2,0},{1,3},{3,1},{4,6},{6,4},{5,7},{7,5},{8,10},{10,8},{9,1... | collective-permute-start | bytes 1769480 | tf_op jit(solution)/shard_map/ppermute | solution.py:245
  10.3 30.9 %collective-permute-start.1 = (f32[192,768]{1,0:T(8,128)S(1)}, f32[192,768]{1,0:T(8,128)S(1)}, u32[]{:S(2)}, u32[]{:S(2)}) collective-permute-start(f32[192,768]{1,0:T(8,128)S(1)} %get-tuple-element.55), channel_id=1, source_target_pairs={{0,4},{4,0},{8,12},{12,8},{16,20},{20,16},{24,28},{28,24},{1,5},{5... | collective-permute-start | bytes 1769480 | tf_op jit(solution)/shard_map/ppermute | solution.py:246
  11.9 29.3 %collective-permute-start.2 = (f32[192,768]{1,0:T(8,128)S(1)}, f32[192,768]{1,0:T(8,128)S(1)}, u32[]{:S(2)}, u32[]{:S(2)}) collective-permute-start(f32[192,768]{1,0:T(8,128)S(1)} %get-tuple-element.55), channel_id=1, source_target_pairs={{0,6},{2,4},{4,2},{6,0},{8,14},{10,12},{12,10},{14,8},{16,22},{18,... | collective-permute-start | bytes 1769480 | tf_op jit(solution)/shard_map/ppermute | solution.py:247
  21.9 21.1 %collective-permute-start.5 = (f32[1,2,96,128]{3,2,1,0:T(8,128)S(1)}, f32[1,2,96,128]{3,2,1,0:T(8,128)S(1)}, u32[]{:S(2)}, u32[]{:S(2)}) collective-permute-start(f32[1,2,96,128]{3,2,1,0:T(8,128)S(1)} %get-tuple-element.102), channel_id=1, source_target_pairs={{0,8},{4,12},{8,24},{12,28},{24,16},{28,20},{16,0},{20,4},{1,9},{5... | collective-permute-start | bytes 294920 | tf_op jit(solution)/shard_map/ppermute | solution.py:263
  43.5 4.5 %collective-permute-start.6 = (f32[2,192,128]{2,1,0:T(8,128)S(1)}, f32[2,192,128]{2,1,0:T(8,128)S(1)}, u32[]{:S(2)}, u32[]{:S(2)}) collective-permute-start(f32[2,192,128]{2,1,0:T(8,128)S(1)} %get-tuple-element.68), channel_id=1, source_target_pairs={{0,1},{1,0},{2,3},{3,2},{4,5},{5,4},{6,7},{7,6},{8,9},{9,8},{10,11... | collective-permute-start | bytes 589832 | tf_op jit(solution)/shard_map/ppermute | solution.py:291
  43.6 9.3 %collective-permute-start.7 = (f32[1,2,96,256]{3,2,1,0:T(8,128)S(1)}, f32[1,2,96,256]{3,2,1,0:T(8,128)S(1)}, u32[]{:S(2)}, u32[]{:S(2)}) collective-permute-start(f32[1,2,96,256]{3,2,1,0:T(8,128)S(1)} %get-tuple-element.105), channel_id=1, source_target_pairs={{0,8},{4,12},{8,24},{12,28},{24,16},{28,20},{16,0},{20,4},{1,9},{5... | collective-permute-start | bytes 589832 | tf_op jit(solution)/shard_map/ppermute | solution.py:263
  53.4 3.4 %collective-permute-start.8 = (f32[2,192,256]{2,1,0:T(8,128)S(1)}, f32[2,192,256]{2,1,0:T(8,128)S(1)}, u32[]{:S(2)}, u32[]{:S(2)}) collective-permute-start(f32[2,192,256]{2,1,0:T(8,128)S(1)} %get-tuple-element.75), channel_id=1, source_target_pairs={{0,1},{1,0},{2,3},{3,2},{4,5},{5,4},{6,7},{7,6},{8,9},{9,8},{10,11... | collective-permute-start | bytes 1179656 | tf_op jit(solution)/shard_map/ppermute | solution.py:291
  53.4 8.5 %collective-permute-start.9 = (f32[1,2,96,256]{3,2,1,0:T(8,128)S(1)}, f32[1,2,96,256]{3,2,1,0:T(8,128)S(1)}, u32[]{:S(2)}, u32[]{:S(2)}) collective-permute-start(f32[1,2,96,256]{3,2,1,0:T(8,128)S(1)} %get-tuple-element.104), channel_id=1, source_target_pairs={{0,8},{4,12},{8,24},{12,28},{24,16},{28,20},{16,0},{20,4},{1,9},{5... | collective-permute-start | bytes 589832 | tf_op jit(solution)/shard_map/ppermute | solution.py:263
  62.4 3.1 %collective-permute-start.10 = (f32[2,192,256]{2,1,0:T(8,128)S(1)}, f32[2,192,256]{2,1,0:T(8,128)S(1)}, u32[]{:S(2)}, u32[]{:S(2)}) collective-permute-start(f32[2,192,256]{2,1,0:T(8,128)S(1)} %get-tuple-element.82), channel_id=1, source_target_pairs={{0,1},{1,0},{2,3},{3,2},{4,5},{5,4},{6,7},{7,6},{8,9},{9,8},{10,11... | collective-permute-start | bytes 1179656 | tf_op jit(solution)/shard_map/ppermute | solution.py:291
  62.5 8.2 %collective-permute-start.11 = (f32[1,2,96,256]{3,2,1,0:T(8,128)S(1)}, f32[1,2,96,256]{3,2,1,0:T(8,128)S(1)}, u32[]{:S(2)}, u32[]{:S(2)}) collective-permute-start(f32[1,2,96,256]{3,2,1,0:T(8,128)S(1)} %get-tuple-element.103), channel_id=1, source_target_pairs={{0,8},{4,12},{8,24},{12,28},{24,16},{28,20},{16,0},{20,4},{1,9},{5... | collective-permute-start | bytes 589832 | tf_op jit(solution)/shard_map/ppermute | solution.py:263
  71.1 3.0 %collective-permute-start.12 = (f32[2,192,256]{2,1,0:T(8,128)S(1)}, f32[2,192,256]{2,1,0:T(8,128)S(1)}, u32[]{:S(2)}, u32[]{:S(2)}) collective-permute-start(f32[2,192,256]{2,1,0:T(8,128)S(1)} %get-tuple-element.89), channel_id=1, source_target_pairs={{0,1},{1,0},{2,3},{3,2},{4,5},{5,4},{6,7},{7,6},{8,9},{9,8},{10,11... | collective-permute-start | bytes 1179656 | tf_op jit(solution)/shard_map/ppermute | solution.py:291
  71.2 6.1 %collective-permute-start.13 = (f32[1,2,96,128]{3,2,1,0:T(8,128)S(1)}, f32[1,2,96,128]{3,2,1,0:T(8,128)S(1)}, u32[]{:S(2)}, u32[]{:S(2)}) collective-permute-start(f32[1,2,96,128]{3,2,1,0:T(8,128)S(1)} %get-tuple-element.101), channel_id=1, source_target_pairs={{0,8},{4,12},{8,24},{12,28},{24,16},{28,20},{16,0},{20,4},{1,9},{5... | collective-permute-start | bytes 294920 | tf_op jit(solution)/shard_map/ppermute | solution.py:263
  77.8 4.2 %collective-permute-start.14 = (f32[2,192,128]{2,1,0:T(8,128)S(1)}, f32[2,192,128]{2,1,0:T(8,128)S(1)}, u32[]{:S(2)}, u32[]{:S(2)}) collective-permute-start(f32[2,192,128]{2,1,0:T(8,128)S(1)} %get-tuple-element.96), channel_id=1, source_target_pairs={{0,1},{1,0},{2,3},{3,2},{4,5},{5,4},{6,7},{7,6},{8,9},{9,8},{10,11... | collective-permute-start | bytes 589832 | tf_op jit(solution)/shard_map/ppermute | solution.py:291
  77.9 18.4 %collective-permute-start.16 = (f32[192,256]{1,0:T(8,128)S(1)}, f32[192,256]{1,0:T(8,128)S(1)}, u32[]{:S(2)}, u32[]{:S(2)}) collective-permute-start(f32[192,256]{1,0:T(8,128)S(1)} %get-tuple-element.79), channel_id=1, source_target_pairs={{0,4},{4,0},{8,12},{12,8},{16,20},{20,16},{24,28},{28,24},{1,5},{5... | collective-permute-start | bytes 589832 | tf_op jit(solution)/shard_map/ppermute | solution.py:297
  79.5 16.8 %collective-permute-start.17 = (f32[192,256]{1,0:T(8,128)S(1)}, f32[192,256]{1,0:T(8,128)S(1)}, u32[]{:S(2)}, u32[]{:S(2)}) collective-permute-start(f32[192,256]{1,0:T(8,128)S(1)} %get-tuple-element.86), channel_id=1, source_target_pairs={{0,4},{4,0},{8,12},{12,8},{16,20},{20,16},{24,28},{28,24},{1,5},{5... | collective-permute-start | bytes 589832 | tf_op jit(solution)/shard_map/ppermute | solution.py:297
  80.0 16.3 %collective-permute-start.18 = (f32[192,256]{1,0:T(8,128)S(1)}, f32[192,256]{1,0:T(8,128)S(1)}, u32[]{:S(2)}, u32[]{:S(2)}) collective-permute-start(f32[192,256]{1,0:T(8,128)S(1)} %get-tuple-element.93), channel_id=1, source_target_pairs={{0,4},{4,0},{8,12},{12,8},{16,20},{20,16},{24,28},{28,24},{1,5},{5... | collective-permute-start | bytes 589832 | tf_op jit(solution)/shard_map/ppermute | solution.py:297
  81.5 14.8 %collective-permute-start.15 = (f32[192,128]{1,0:T(8,128)S(1)}, f32[192,128]{1,0:T(8,128)S(1)}, u32[]{:S(2)}, u32[]{:S(2)}) collective-permute-start(f32[192,128]{1,0:T(8,128)S(1)} %get-tuple-element.72), channel_id=1, source_target_pairs={{0,4},{4,0},{8,12},{12,8},{16,20},{20,16},{24,28},{28,24},{1,5},{5... | collective-permute-start | bytes 294920 | tf_op jit(solution)/shard_map/ppermute | solution.py:297
  82.0 15.8 %collective-permute-start.19 = (f32[192,128]{1,0:T(8,128)S(1)}, f32[192,128]{1,0:T(8,128)S(1)}, u32[]{:S(2)}, u32[]{:S(2)}) collective-permute-start(f32[192,128]{1,0:T(8,128)S(1)} %get-tuple-element.98), channel_id=1, source_target_pairs={{0,4},{4,0},{8,12},{12,8},{16,20},{20,16},{24,28},{28,24},{1,5},{5... | collective-permute-start | bytes 294920 | tf_op jit(solution)/shard_map/ppermute | solution.py:297
  98.5 1.2 %collective-permute-start.20 = (f32[1,1024]{1,0:T(1,128)S(1)}, f32[1,1024]{1,0:T(1,128)S(1)}, u32[]{:S(2)}, u32[]{:S(2)}) collective-permute-start(f32[1,1024]{1,0:T(1,128)S(1)} %get-tuple-element.99), channel_id=1, source_target_pairs={{0,1},{1,0},{2,3},{3,2},{4,5},{5,4},{6,7},{7,6},{8,9},{9,8},{10,11... | collective-permute-start | bytes 12296 | tf_op jit(solution)/shard_map/ppermute | solution.py:46
  99.8 3.6 %collective-permute-start.21 = (f32[1,1024]{1,0:T(1,128)S(1)}, f32[1,1024]{1,0:T(1,128)S(1)}, u32[]{:S(2)}, u32[]{:S(2)}) collective-permute-start(f32[1,1024]{1,0:T(1,128)S(1)} %add.12), channel_id=1, source_target_pairs={{0,4},{4,0},{8,12},{12,8},{16,20},{20,16},{24,28},{28,24},{1,5},{5... | collective-permute-start | bytes 12296 | tf_op jit(solution)/shard_map/ppermute | solution.py:46
  103.4 3.6 %collective-permute-start.22 = (f32[1,1024]{1,0:T(1,128)S(1)}, f32[1,1024]{1,0:T(1,128)S(1)}, u32[]{:S(2)}, u32[]{:S(2)}) collective-permute-start(f32[1,1024]{1,0:T(1,128)S(1)} %add.13), channel_id=1, source_target_pairs={{0,8},{4,12},{8,0},{12,4},{16,24},{20,28},{24,16},{28,20},{1,9},{5... | collective-permute-start | bytes 12296 | tf_op jit(solution)/shard_map/ppermute | solution.py:46
  107.0 4.8 %collective-permute-start.23 = (f32[1,1024]{1,0:T(1,128)S(1)}, f32[1,1024]{1,0:T(1,128)S(1)}, u32[]{:S(2)}, u32[]{:S(2)}) collective-permute-start(f32[1,1024]{1,0:T(1,128)S(1)} %add.14), channel_id=1, source_target_pairs={{0,16},{4,20},{8,24},{12,28},{16,0},{20,4},{24,8},{28,12},{1,17},{... | collective-permute-start | bytes 12296 | tf_op jit(solution)/shard_map/ppermute | solution.py:46
  (4 other events, 45.3 us)
